TPU v7x, 128 devices: a whole 4x4x4 slice. The times are simulated.
128 devices in a mesh: seq: 16 (over x_lo, z, core), tensor: 8 (over y, x_hi).
Axes of the slice: x: 4 (x_hi: 2, x_lo: 2; x = x_hi * 2 + x_lo), y: 4, z: 4, core: 2. Of those that a mesh axis runs over, the one named last changes fastest.
Arguments:
- tokens: bfloat16 [2048, 8192], P('seq', 'tensor'), may hold values from -2000 to 2000
- cotangent: bfloat16 [2048, 8192], P('seq', 'tensor'), may hold values from -6 to 6
- gain: float32 [8192], P('tensor'), may hold values from 0.25 to 1.75
- w_gate: bfloat16 [8192, 14336], P('tensor', 'seq'), may hold values from -0.0625 to 0.0625
- w_up: bfloat16 [8192, 14336], P('tensor', 'seq'), may hold values from -0.0625 to 0.0625
- w_down: bfloat16 [14336, 8192], P('seq', 'tensor'), may hold values from -0.046875 to 0.046875
- probe: bfloat16 [8192, 14336], P('tensor', 'seq'), may hold values from -1 to 1, as said below
Outputs:
- hessian_probe: float32 [8192, 14336], P('tensor', 'seq')
Inputs may be any that keep to these rules, and one draw needn't show every extreme that they name: `probe`: every entry is +1 or -1.
All inputs are finite; a program needn't handle non-finite values.
Results may differ from a plain program's by a relative error of at most 0.024.
Values may be sent and summed in bfloat16 or wider, within the bound.
No kernel may reach another device: no remote copies, remote signals or barrier semaphores. Data moves between devices by JAX's collectives and lax.ppermute only.
A program may use at most 128 MiB of HBM per device.

v0:
```python
import jax
import jax.numpy as jnp
from jax import lax
from jax.sharding import PartitionSpec as P

D = 8192


epsilon = 1e-05


def second_factor(pre_gate, pre_up, tangent, upstream):
    sigmoid_gate = jax.nn.sigmoid(pre_gate)
    curvature = sigmoid_gate * (1.0 - sigmoid_gate) * (2.0 + pre_gate * (1.0 - 2.0 * sigmoid_gate))
    return (upstream * pre_up * curvature * tangent).astype(jnp.bfloat16)


def body(tokens, cotangent, gain, w_gate, w_up, w_down, probe):
    gathered, upstream_rows = (
        lax.all_gather(tokens, "seq", axis=0, tiled=True),
        lax.all_gather(cotangent, "seq", axis=0, tiled=True),
    )
    values = gathered.astype(jnp.float32)
    squares = lax.psum(jnp.sum(values * values, axis=1), "tensor")
    inverse = lax.rsqrt(squares / D + epsilon)
    normed = (values * inverse[:, None] * gain[None, :]).astype(jnp.bfloat16)
    total_tokens = normed.shape[0]
    unit_count = w_gate.shape[1]
    norm_block = normed
    outputs = [
        jnp.dot(norm_block, weight, preferred_element_type=jnp.float32)
        for weight in (w_gate, w_up, probe)
    ]
    outputs.append(
        lax.dot_general(
            upstream_rows, w_down, (((1,), (1,)), ((), ())), preferred_element_type=jnp.float32
        )
    )
    summed = lax.psum_scatter(
        jnp.concatenate(outputs, axis=1).astype(jnp.bfloat16),
        "tensor",
        scatter_dimension=0,
        tiled=True,
    ).astype(jnp.float32)
    second = second_factor(
        summed[:, :unit_count],
        summed[:, unit_count : 2 * unit_count],
        summed[:, 2 * unit_count : 3 * unit_count],
        summed[:, 3 * unit_count :],
    )
    norm_block = normed
    product = lax.dot_general(
        norm_block,
        lax.all_gather(second, "tensor", axis=0, tiled=True),
        (((0,), (0,)), ((), ())),
        preferred_element_type=jnp.float32,
    )
    return product / total_tokens


def solution(mesh):
    return jax.shard_map(
        body,
        mesh=mesh,
        in_specs=(
            P("seq", "tensor"),
            P("seq", "tensor"),
            P("tensor"),
            P("tensor", "seq"),
            P("tensor", "seq"),
            P("seq", "tensor"),
            P("tensor", "seq"),
        ),
        out_specs=P("tensor", "seq"),
        check_vma=False,
    )
```

profile of v0, /device:TPU:0, one launch (start us, length us, event | category | flops | bytes accessed | tf_op | source)
XLA Modules:
  0.0 385.9 jit_solution(4910168652188962719)
XLA Ops:
  6.5 0.0 copy-start
  6.5 0.0 copy-start.7
  6.5 0.0 all-gather.4.cloned.1.call-start
  6.5 0.7 all-gather.4.cloned.1.call-update
  7.3 0.0 all-gather.6.cloned.1.call-start
  7.3 0.7 all-gather.6.cloned.1.call-update
  8.0 0.0 reduce-scatter.2.cloned.1.call-start
  8.1 40.8 %all-gather.4.cloned.1.call-done = bf16[2048,1024]{1,0:T(8,128)(2,1)} async-done(((bf16[128,1024]{1,0:T(8,128)(2,1)}), bf16[2048,1024]{1,0:T(8,128)(2,1)}) %all-gather.4.cloned.1.call-update) | async-done | bytes 4194320 | tf_op jit(solution)/shard_map/all_gather | solution.py:20
  48.9 3.1 fusion
  52.0 24.9 %psum.7 = f32[2048]{0:T(1024)S(1)} all-reduce(f32[2048]{0:T(1024)S(1)} %fusion), channel_id=1, replica_groups=mesh['seq'=16,'tensor'=8] {'tensor'}, use_global_device_ids=true, to_apply=%region_1.0 | all-reduce | flops 2048 | bytes 16384 | tf_op jit(solution)/shard_map/psum | solution.py:24
  76.9 0.0 copy-done
  76.9 0.0 copy-done.7
  76.9 0.0 copy-start.1
  77.0 0.0 copy-start.5
  77.0 8.5 %convolution_convert_fusion.2 = bf16[2048,896]{0,1:T(8,128)(2,1)} fusion(bf16[1024,896]{1,0:T(8,128)(2,1)S(1)} %copy-done, bf16[2048,1024]{1,0:T(8,128)(2,1)} %all-gather.4.cloned.1.call-done, f32[1024]{0:T(1024)S(1)} %copy-done.7, f32[2048]{0:T(1024)S(1)} %add_rsqrt_fusion), kind=kOutput, calls=%fused_computation.8 | convolution fusion | flops 3768320000 | bytes 9711616 | tf_op jit(solution)/shard_map/dot_general | solution.py:31
  85.4 0.0 copy-done.1
  85.4 0.0 copy-done.5
  85.4 0.0 copy-start.6
  85.4 6.0 %convolution_convert_fusion.1 = bf16[2048,896]{0,1:T(8,128)(2,1)} fusion(bf16[1024,896]{1,0:T(8,128)(2,1)S(1)} %copy-done.5, bf16[2048,1024]{1,0:T(8,128)(2,1)S(1)} %copy-done.1, f32[1024]{0:T(1024)S(1)} %copy-done.7, f32[2048]{0:T(1024)S(1)} %add_rsqrt_fusion), kind=kOutput, calls=%fused_computation.7 | convolution fusion | flops 3768320000 | bytes 9711616 | tf_op jit(solution)/shard_map/dot_general | solution.py:31
  91.5 0.0 copy-done.6
  91.5 5.9 %convolution_convert_fusion.3 = bf16[2048,896]{0,1:T(8,128)(2,1)} fusion(bf16[1024,896]{1,0:T(8,128)(2,1)S(1)} %copy-done.6, bf16[2048,1024]{1,0:T(8,128)(2,1)S(1)} %copy-done.1, f32[1024]{0:T(1024)S(1)} %copy-done.7, f32[2048]{0:T(1024)S(1)} %add_rsqrt_fusion), kind=kOutput, calls=%fused_computation.9 | convolution fusion | flops 3768320000 | bytes 9711616 | tf_op jit(solution)/shard_map/dot_general | solution.py:31
  97.3 0.0 all-gather.6.cloned.1.call-done
  97.4 0.0 copy-start.2
  97.4 0.0 copy-start.3
  97.4 0.0 copy-start.4
  97.4 6.9 %convolution_convert_fusion = bf16[2048,896]{0,1:T(8,128)(2,1)S(1)} fusion(bf16[2048,1024]{1,0:T(8,128)(2,1)} %all-gather.6.cloned.1.call-done, bf16[896,1024]{1,0:T(8,128)(2,1)} %param.12), kind=kOutput, calls=%fused_computation.6 | convolution fusion | flops 3759931392 | bytes 9699328 | tf_op jit(solution)/shard_map/dot_general | solution.py:35
  104.3 0.0 copy-done.2
  104.3 0.0 copy-done.3
  104.3 0.0 copy-done.4
  104.3 31.3 %pad_maximum_fusion = bf16[2048,3584]{0,1:T(8,128)(2,1)} fusion(bf16[2048,896]{0,1:T(8,128)(2,1)S(1)} %convolution_convert_fusion, bf16[2048,896]{0,1:T(8,128)(2,1)S(1)} %copy-done.3, bf16[2048,896]{0,1:T(8,128)(2,1)S(1)} %copy-done.2, bf16[2048,896]{0,1:T(8,128)(2,1)S(1)} %copy-done.4), kind=kLoop, calls=%fused_computation | loop fusion | flops 58720256 | bytes 29360128 | tf_op jit(solution)/shard_map/concatenate | solution.py:40
  135.6 0.0 reduce-scatter.2.cloned.1.call-update
  135.6 0.0 all-gather.8.cloned.1.call-start
  135.7 164.5 %reduce-scatter.2.cloned.1.call-done = bf16[256,3584]{0,1:T(8,128)(2,1)} async-done(((bf16[2048,3584]{0,1:T(8,128)(2,1)}), bf16[256,3584]{0,1:T(8,128)(2,1)}) %reduce-scatter.2.cloned.1.call-update) | async-done | bytes 1835024 | tf_op jit(solution)/shard_map/reduce_scatter | solution.py:39
  300.1 1.8 convert_element_type.15
  301.9 1.2 fusion.6
  303.1 0.0 all-gather.8.cloned.1.call-update
  303.2 66.1 %all-gather.8.cloned.1.call-done = bf16[2048,896]{0,1:T(8,128)(2,1)} async-done(((bf16[256,896]{0,1:T(8,128)(2,1)}), bf16[2048,896]{0,1:T(8,128)(2,1)}) %all-gather.8.cloned.1.call-update) | async-done | bytes 3670032 | tf_op jit(solution)/shard_map/all_gather | solution.py:54
  369.3 10.1 %convolution_multiply_fusion = f32[1024,896]{1,0:T(8,128)} fusion(bf16[2048,896]{0,1:T(8,128)(2,1)} %all-gather.8.cloned.1.call-done, bf16[2048,1024]{1,0:T(8,128)(2,1)} %all-gather.4.cloned.1.call-done, f32[1024]{0:T(1024)S(1)} %copy-done.7, f32[2048]{0:T(1024)S(1)} %add_rsqrt_fusion), kind=kOutput, calls=%fused_computation.10 | convolution fusion | flops 3767402496 | bytes 11546624 | tf_op jit(solution)/shard_map/dot_general | solution.py:52
  (1 shorter events, 0.0 us)
Async XLA Ops:
  6.5 70.4 %copy-start = (bf16[1024,896]{1,0:T(8,128)(2,1)S(1)}, bf16[1024,896]{1,0:T(8,128)(2,1)}, u32[]{:S(2)}) copy-start(bf16[1024,896]{1,0:T(8,128)(2,1)} %param.11) | copy-start | bytes 5505028
  6.5 70.4 %copy-start.7 = (f32[1024]{0:T(1024)S(1)}, f32[1024]{0:T(1024)}, u32[]{:S(2)}) copy-start(f32[1024]{0:T(1024)} %param.9) | copy-start | bytes 12292
  6.5 42.4 %all-gather.4.cloned.1.call-start = ((), (), s32[]{:S(2)}) async-start(), calls=%async_computation.1 | async-start | bytes 4456448 | tf_op jit(solution)/shard_map/all_gather | solution.py:20
  7.3 90.1 %all-gather.6.cloned.1.call-start = ((), (), s32[]{:S(2)}) async-start(), calls=%async_computation.2 | async-start | bytes 4456448 | tf_op jit(solution)/shard_map/all_gather | solution.py:21
  8.0 292.1 %reduce-scatter.2.cloned.1.call-start = ((), (), s32[]{:S(2)}) async-start(), calls=%async_computation.3 | async-start | bytes 16515072 | tf_op jit(solution)/shard_map/reduce_scatter | solution.py:39
  76.9 8.5 %copy-start.1 = (bf16[2048,1024]{1,0:T(8,128)(2,1)S(1)}, bf16[2048,1024]{1,0:T(8,128)(2,1)}, u32[]{:S(2)}) copy-start(bf16[2048,1024]{1,0:T(8,128)(2,1)} %all-gather.4.cloned.1.call-done) | copy-start | bytes 12582916
  77.0 8.5 %copy-start.5 = (bf16[1024,896]{1,0:T(8,128)(2,1)S(1)}, bf16[1024,896]{1,0:T(8,128)(2,1)}, u32[]{:S(2)}) copy-start(bf16[1024,896]{1,0:T(8,128)(2,1)} %param.13) | copy-start | bytes 5505028
  85.4 6.0 %copy-start.6 = (bf16[1024,896]{1,0:T(8,128)(2,1)S(1)}, bf16[1024,896]{1,0:T(8,128)(2,1)}, u32[]{:S(2)}) copy-start(bf16[1024,896]{1,0:T(8,128)(2,1)} %param.10) | copy-start | bytes 5505028
  97.4 6.9 %copy-start.2 = (bf16[2048,896]{0,1:T(8,128)(2,1)S(1)}, bf16[2048,896]{0,1:T(8,128)(2,1)}, u32[]{:S(2)}) copy-start(bf16[2048,896]{0,1:T(8,128)(2,1)} %convolution_convert_fusion.2) | copy-start | bytes 11010052
  97.4 6.9 %copy-start.3 = (bf16[2048,896]{0,1:T(8,128)(2,1)S(1)}, bf16[2048,896]{0,1:T(8,128)(2,1)}, u32[]{:S(2)}) copy-start(bf16[2048,896]{0,1:T(8,128)(2,1)} %convolution_convert_fusion.1) | copy-start | bytes 11010052
  97.4 6.9 %copy-start.4 = (bf16[2048,896]{0,1:T(8,128)(2,1)S(1)}, bf16[2048,896]{0,1:T(8,128)(2,1)}, u32[]{:S(2)}) copy-start(bf16[2048,896]{0,1:T(8,128)(2,1)} %convolution_convert_fusion.3) | copy-start | bytes 11010052
  135.6 233.7 %all-gather.8.cloned.1.call-start = ((), (), s32[]{:S(2)}) async-start(), calls=%async_computation.4 | async-start | bytes 4128768 | tf_op jit(solution)/shard_map/all_gather | solution.py:54
Sparse Core Ops, SparseCore 0:
  9.0 39.8 all-gather.3
  50.6 37.3 all-gather.5
  135.7 164.3 reduce-scatter.1
  303.3 65.9 all-gather.7
where the time goes:
time: 386 us
  waiting for transfers between devices  273 us (71%)
  other arithmetic  37.4 us (10%)
  matrix products  37.4 us (10%)
  blocking collectives  24.9 us (6%)
  between operations  13.2 us (3%)
    reduce_scatter x1, waiting for transfers between devices, body(): lax.psum_scatter(jnp.concatenate(outputs, axis=1).astype(jnp.bfloat16), '...  164 us
    all_gather x1, waiting for transfers between devices, body(): lax.all_gather(second, 'tensor', axis=0, tiled=True)  66.1 us
    all_gather x1, waiting for transfers between devices, body(): lax.all_gather(tokens, 'seq', axis=0, tiled=True)  40.8 us
    concatenate x1, other arithmetic, body(): jnp.concatenate(outputs, axis=1).astype(jnp.bfloat16)  31.3 us
    psum x1, blocking collectives, body(): squares = lax.psum(jnp.sum(values * values, axis=1), 'tensor')  24.9 us
    dot_general x3, matrix products, body(): jnp.dot(norm_block, weight, preferred_element_type=jnp.float32)  20.4 us
    dot_general x1, matrix products, body(): lax.dot_general(norm_block, lax.all_gather(second, 'tensor', axis=0, tile...  10.1 us
  transfers between devices with their start and end apart: 4, of which 3 were waited for; matrix products, arithmetic and copies ran while one was open for 6% of the time, Pallas kernels for 0%

commit v1 on v0

v1 whole, which is shorter than its diff:
```python
import jax
import jax.numpy as jnp
from jax import lax
from jax.sharding import PartitionSpec as P

D = 8192


epsilon = 1e-05


def second_factor(pre_gate, pre_up, tangent, upstream):
    sigmoid_gate = jax.nn.sigmoid(pre_gate)
    curvature = sigmoid_gate * (1.0 - sigmoid_gate) * (2.0 + pre_gate * (1.0 - 2.0 * sigmoid_gate))
    return (upstream * pre_up * curvature * tangent).astype(jnp.bfloat16)


def body(tokens, cotangent, gain, w_gate, w_up, w_down, probe):
    upstream_rows = lax.all_gather(cotangent, "seq", axis=0, tiled=True)
    values = tokens.astype(jnp.float32)
    squares = lax.psum(jnp.sum(values * values, axis=1), "tensor")
    inverse = lax.rsqrt(squares / D + epsilon)
    normed_local = (values * inverse[:, None] * gain[None, :]).astype(jnp.bfloat16)
    normed = lax.all_gather(normed_local, "seq", axis=0, tiled=True)
    total_tokens = normed.shape[0]
    parts = [
        jnp.dot(normed, weight, preferred_element_type=jnp.float32).astype(jnp.bfloat16)
        for weight in (w_gate, w_up, probe)
    ]
    parts.append(
        lax.dot_general(
            upstream_rows, w_down, (((1,), (1,)), ((), ())), preferred_element_type=jnp.float32
        ).astype(jnp.bfloat16)
    )
    summed = [
        lax.psum_scatter(p, "tensor", scatter_dimension=0, tiled=True).astype(jnp.float32)
        for p in parts
    ]
    second = second_factor(*summed)
    product = lax.dot_general(
        normed,
        lax.all_gather(second, "tensor", axis=0, tiled=True),
        (((0,), (0,)), ((), ())),
        preferred_element_type=jnp.float32,
    )
    return product / total_tokens


def solution(mesh):
    return jax.shard_map(
        body,
        mesh=mesh,
        in_specs=(
            P("seq", "tensor"),
            P("seq", "tensor"),
            P("tensor"),
            P("tensor", "seq"),
            P("tensor", "seq"),
            P("seq", "tensor"),
            P("tensor", "seq"),
        ),
        out_specs=P("tensor", "seq"),
        check_vma=False,
    )
```

time: 386 us -> 514 us (1.33)
  waiting for transfers between devices: 273 us -> 425 us
  other arithmetic: 37.4 us -> 5.65 us
  matrix products: 37.4 us -> 45.3 us
    reduce_scatter x1 -> x4, waiting for transfers between devices: 164 us -> 314 us  [body(): lax.psum_scatter(p, 'tensor', scatter_dimension=0, tiled=True)]
    concatenate x1 -> x0, other arithmetic: 31.3 us -> none  [body(): jnp.concatenate(outputs, axis=1).astype(jnp.bfloat16)]
    dot_general x4, matrix products: 30.5 us -> 37.2 us  [the longest x3 27.4 us: body(): jnp.dot(normed, weight, preferred_element_type=jnp.float32)]
  transfers between devices with their start and end apart: 4 -> 7, of which waited for: 3 -> 7; matrix products, arithmetic and copies ran while one was open for 6% -> 7% of each run, Pallas kernels for 0% -> 0%
where the time goes in v1:
time: 514 us
  waiting for transfers between devices  425 us (83%)
  matrix products  45.3 us (9%)
  blocking collectives  24.7 us (5%)
  between operations  13.5 us (3%)
  other arithmetic  5.65 us (1%)
    reduce_scatter x4, waiting for transfers between devices, body(): lax.psum_scatter(p, 'tensor', scatter_dimension=0, tiled=True)  314 us
    all_gather x1, waiting for transfers between devices, body(): lax.all_gather(second, 'tensor', axis=0, tiled=True)  65.6 us
    all_gather x1, waiting for transfers between devices, body(): normed = lax.all_gather(normed_local, 'seq', axis=0, tiled=True)  30.5 us
    dot_general x3, matrix products, body(): jnp.dot(normed, weight, preferred_element_type=jnp.float32)  27.4 us
    psum x1, blocking collectives, body(): squares = lax.psum(jnp.sum(values * values, axis=1), 'tensor')  24.7 us
    all_gather x1, waiting for transfers between devices, body(): upstream_rows = lax.all_gather(cotangent, 'seq', axis=0, tiled=True)  14 us
  transfers between devices with their start and end apart: 7, of which 7 were waited for; matrix products, arithmetic and copies ran while one was open for 7% of the time, Pallas kernels for 0%

profile of v1, /device:TPU:0, one launch (start us, length us, event | category | flops | bytes accessed | tf_op | source)
XLA Modules:
  0.0 514.1 jit_solution(5551802567788721548)
XLA Ops:
  6.5 0.0 copy-start
  6.5 0.0 all-gather.6.cloned.1.call-start
  6.5 0.7 all-gather.6.cloned.1.call-update
  7.3 0.0 all-gather.4.cloned.1.call-start
  7.3 1.1 fusion.8
  8.4 24.7 %psum.7 = f32[128]{0:T(128)S(1)} all-reduce(f32[128]{0:T(128)S(1)} %fusion.8), channel_id=1, replica_groups=mesh['seq'=16,'tensor'=8] {'tensor'}, use_global_device_ids=true, to_apply=%region_1.0 | all-reduce | flops 128 | bytes 1024 | tf_op jit(solution)/shard_map/psum | solution.py:21
  33.1 1.8 fusion.10
  34.9 0.0 all-gather.4.cloned.1.call-update
  34.9 0.0 reduce-scatter.5.cloned.1.call-start
  35.0 14.0 %all-gather.6.cloned.1.call-done = bf16[2048,1024]{1,0:T(8,128)(2,1)} async-done(((bf16[128,1024]{1,0:T(8,128)(2,1)}), bf16[2048,1024]{1,0:T(8,128)(2,1)}) %all-gather.6.cloned.1.call-update) | async-done | bytes 4194320 | tf_op jit(solution)/shard_map/all_gather | solution.py:19
  49.0 0.0 copy-done
  49.0 8.2 %convolution_convert_fusion.3 = bf16[2048,896]{1,0:T(8,128)(2,1)} fusion(bf16[2048,1024]{1,0:T(8,128)(2,1)} %all-gather.6.cloned.1.call-done, bf16[896,1024]{1,0:T(8,128)(2,1)S(1)} %copy-done), kind=kOutput, calls=%fused_computation.3 | convolution fusion | flops 3759931392 | bytes 9699328 | tf_op jit(solution)/shard_map/dot_general | solution.py:31
  57.2 0.0 reduce-scatter.5.cloned.1.call-update
  57.2 0.0 reduce-scatter.11.cloned.1.call-start
  57.2 30.5 %all-gather.4.cloned.1.call-done = bf16[2048,1024]{1,0:T(8,128)(2,1)} async-done(((bf16[128,1024]{1,0:T(8,128)(2,1)}), bf16[2048,1024]{1,0:T(8,128)(2,1)}) %all-gather.4.cloned.1.call-update) | async-done | bytes 4194320 | tf_op jit(solution)/shard_map/all_gather | solution.py:24
  87.7 9.2 %convolution_convert_fusion = bf16[2048,896]{1,0:T(8,128)(2,1)} fusion(bf16[2048,1024]{1,0:T(8,128)(2,1)} %all-gather.4.cloned.1.call-done, bf16[1024,896]{1,0:T(8,128)(2,1)} %param.13), kind=kOutput, calls=%fused_computation | convolution fusion | flops 3759931392 | bytes 9699328 | tf_op jit(solution)/shard_map/dot_general | solution.py:27
  96.9 0.0 reduce-scatter.11.cloned.1.call-update
  97.0 0.0 reduce-scatter.9.cloned.1.call-start
  97.0 9.1 %convolution_convert_fusion.1 = bf16[2048,896]{1,0:T(8,128)(2,1)} fusion(bf16[2048,1024]{1,0:T(8,128)(2,1)} %all-gather.4.cloned.1.call-done, bf16[1024,896]{1,0:T(8,128)(2,1)} %param.10), kind=kOutput, calls=%fused_computation.1 | convolution fusion | flops 3759931392 | bytes 9699328 | tf_op jit(solution)/shard_map/dot_general | solution.py:27
  106.1 0.0 reduce-scatter.9.cloned.1.call-update
  106.2 0.2 reduce-scatter.7.cloned.1.call-start
  106.4 9.1 %convolution_convert_fusion.2 = bf16[2048,896]{1,0:T(8,128)(2,1)} fusion(bf16[2048,1024]{1,0:T(8,128)(2,1)} %all-gather.4.cloned.1.call-done, bf16[1024,896]{1,0:T(8,128)(2,1)} %param.11), kind=kOutput, calls=%fused_computation.2 | convolution fusion | flops 3759931392 | bytes 9699328 | tf_op jit(solution)/shard_map/dot_general | solution.py:27
  115.5 0.0 reduce-scatter.7.cloned.1.call-update
  115.5 0.0 all-gather.8.cloned.1.call-start
  115.6 58.2 %reduce-scatter.5.cloned.1.call-done = bf16[256,896]{1,0:T(8,128)(2,1)} async-done(((bf16[2048,896]{1,0:T(8,128)(2,1)}), bf16[256,896]{1,0:T(8,128)(2,1)}) %reduce-scatter.5.cloned.1.call-update) | async-done | bytes 458768 | tf_op jit(solution)/shard_map/reduce_scatter | solution.py:36
  173.8 85.1 %reduce-scatter.11.cloned.1.call-done = bf16[256,896]{1,0:T(8,128)(2,1)} async-done(((bf16[2048,896]{1,0:T(8,128)(2,1)}), bf16[256,896]{1,0:T(8,128)(2,1)}) %reduce-scatter.11.cloned.1.call-update) | async-done | bytes 458768 | tf_op jit(solution)/shard_map/reduce_scatter | solution.py:36
  258.9 85.1 %reduce-scatter.9.cloned.1.call-done = bf16[256,896]{1,0:T(8,128)(2,1)} async-done(((bf16[2048,896]{1,0:T(8,128)(2,1)}), bf16[256,896]{1,0:T(8,128)(2,1)}) %reduce-scatter.9.cloned.1.call-update) | async-done | bytes 458768 | tf_op jit(solution)/shard_map/reduce_scatter | solution.py:36
  344.0 85.1 %reduce-scatter.7.cloned.1.call-done = bf16[256,896]{1,0:T(8,128)(2,1)} async-done(((bf16[2048,896]{1,0:T(8,128)(2,1)}), bf16[256,896]{1,0:T(8,128)(2,1)}) %reduce-scatter.7.cloned.1.call-update) | async-done | bytes 458768 | tf_op jit(solution)/shard_map/reduce_scatter | solution.py:36
  429.1 2.8 fusion.7
  431.9 0.0 all-gather.8.cloned.1.call-update
  431.9 65.6 %all-gather.8.cloned.1.call-done = bf16[2048,896]{1,0:T(8,128)(2,1)} async-done(((bf16[256,896]{1,0:T(8,128)(2,1)}), bf16[2048,896]{1,0:T(8,128)(2,1)}) %all-gather.8.cloned.1.call-update) | async-done | bytes 3670032 | tf_op jit(solution)/shard_map/all_gather | solution.py:42
  497.6 9.7 %convolution_multiply_fusion = f32[1024,896]{1,0:T(8,128)} fusion(bf16[2048,1024]{1,0:T(8,128)(2,1)} %all-gather.4.cloned.1.call-done, bf16[2048,896]{1,0:T(8,128)(2,1)} %all-gather.8.cloned.1.call-done), kind=kOutput, calls=%fused_computation.4 | convolution fusion | flops 3759013888 | bytes 11534336 | tf_op jit(solution)/shard_map/dot_general | solution.py:40
  (1 shorter events, 0.0 us)
Async XLA Ops:
  6.5 42.5 %copy-start = (bf16[896,1024]{1,0:T(8,128)(2,1)S(1)}, bf16[896,1024]{1,0:T(8,128)(2,1)}, u32[]{:S(2)}) copy-start(bf16[896,1024]{1,0:T(8,128)(2,1)} %param.12) | copy-start | bytes 5505028
  6.5 42.5 %all-gather.6.cloned.1.call-start = ((), (), s32[]{:S(2)}) async-start(), calls=%async_computation.5 | async-start | bytes 4456448 | tf_op jit(solution)/shard_map/all_gather | solution.py:19
  7.3 80.5 %all-gather.4.cloned.1.call-start = ((), (), s32[]{:S(2)}) async-start(), calls=%async_computation.4 | async-start | bytes 4456448 | tf_op jit(solution)/shard_map/all_gather | solution.py:24
  34.9 138.8 %reduce-scatter.5.cloned.1.call-start = ((), (), s32[]{:S(2)}) async-start(), calls=%async_computation.6 | async-start | bytes 4128768 | tf_op jit(solution)/shard_map/reduce_scatter | solution.py:36
  57.2 201.7 %reduce-scatter.11.cloned.1.call-start = ((), (), s32[]{:S(2)}) async-start(), calls=%async_computation.9 | async-start | bytes 4128768 | tf_op jit(solution)/shard_map/reduce_scatter | solution.py:36
  97.0 247.1 %reduce-scatter.9.cloned.1.call-start = ((), (), s32[]{:S(2)}) async-start(), calls=%async_computation.8 | async-start | bytes 4128768 | tf_op jit(solution)/shard_map/reduce_scatter | solution.py:36
  106.2 323.0 %reduce-scatter.7.cloned.1.call-start = ((), (), s32[]{:S(2)}) async-start(), calls=%async_computation.7 | async-start | bytes 4128768 | tf_op jit(solution)/shard_map/reduce_scatter | solution.py:36
  115.5 382.0 %all-gather.8.cloned.1.call-start = ((), (), s32[]{:S(2)}) async-start(), calls=%async_computation.10 | async-start | bytes 4128768 | tf_op jit(solution)/shard_map/all_gather | solution.py:42
Sparse Core Ops, SparseCore 0:
  9.0 39.9 all-gather.5
  50.7 36.9 all-gather.3
  91.6 82.0 reduce-scatter.4
  177.5 81.3 reduce-scatter.10
  262.6 81.3 reduce-scatter.8
  347.8 81.3 reduce-scatter.6
  432.0 65.4 all-gather.7

commit v2 on v1

v2 whole, which is shorter than its diff:
```python
import functools

import jax
import jax.numpy as jnp
from jax import lax
from jax.experimental import pallas as pl
from jax.experimental.pallas import tpu as pltpu
from jax.sharding import PartitionSpec as P

D = 8192
CHUNKS = 2

epsilon = 1e-05


def second_factor(pre_gate, pre_up, tangent, upstream):
    sigmoid_gate = jax.nn.sigmoid(pre_gate)
    curvature = sigmoid_gate * (1.0 - sigmoid_gate) * (2.0 + pre_gate * (1.0 - 2.0 * sigmoid_gate))
    return (upstream * pre_up * curvature * tangent).astype(jnp.bfloat16)


def products_kernel(n_ref, c_ref, wg_ref, wu_ref, pr_ref, wd_ref, o_ref):
    f = wg_ref.shape[1]
    n = n_ref[...]
    for p, w_ref in enumerate((wg_ref, wu_ref, pr_ref)):
        o_ref[0, :, p * f:(p + 1) * f] = jnp.dot(
            n, w_ref[...], preferred_element_type=jnp.float32
        ).astype(o_ref.dtype)
    o_ref[0, :, 3 * f:4 * f] = lax.dot_general(
        c_ref[...], wd_ref[...], (((1,), (1,)), ((), ())), preferred_element_type=jnp.float32
    ).astype(o_ref.dtype)


def products(normed, cot, w_gate, w_up, probe, w_down, blocks):
    rows, width = normed.shape
    f = w_gate.shape[1]
    tm = rows // blocks
    full = lambda shape: pl.BlockSpec(shape, lambda i: (0, 0))
    return pl.pallas_call(
        products_kernel,
        out_shape=jax.ShapeDtypeStruct((blocks, tm, 4 * f), jnp.bfloat16),
        grid=(blocks,),
        in_specs=[
            pl.BlockSpec((tm, width), lambda i: (i, 0)),
            pl.BlockSpec((tm, width), lambda i: (i, 0)),
            full(w_gate.shape),
            full(w_up.shape),
            full(probe.shape),
            full(w_down.shape),
        ],
        out_specs=pl.BlockSpec((1, tm, 4 * f), lambda i: (i, 0, 0)),
        compiler_params=pltpu.CompilerParams(vmem_limit_bytes=48 * 1024 * 1024),
        cost_estimate=pl.CostEstimate(
            flops=2 * rows * width * f * 4,
            transcendentals=0,
            bytes_accessed=2 * (2 * rows * width + 4 * width * f + rows * 4 * f),
        ),
    )(normed, cot, w_gate, w_up, probe, w_down)


def body(tokens, cotangent, gain, w_gate, w_up, w_down, probe):
    n_tensor = lax.axis_size("tensor")
    values = tokens.astype(jnp.float32)
    squares = lax.psum(jnp.sum(values * values, axis=1), "tensor")
    inverse = lax.rsqrt(squares / D + epsilon)
    normed_local = (values * inverse[:, None] * gain[None, :]).astype(jnp.bfloat16)
    local_rows = tokens.shape[0]
    step = local_rows // CHUNKS
    unit_count = w_gate.shape[1]
    total = None
    total_tokens = 0
    for c in range(CHUNKS):
        rows = slice(c * step, (c + 1) * step)
        cot_c = lax.all_gather(cotangent[rows], "seq", axis=0, tiled=True)
        normed_c = lax.all_gather(normed_local[rows], "seq", axis=0, tiled=True)
        total_tokens += normed_c.shape[0]
        parts = products(normed_c, cot_c, w_gate, w_up, probe, w_down, n_tensor)
        received = lax.all_to_all(parts, "tensor", 0, 0, tiled=True)
        summed = jnp.sum(received.astype(jnp.float32), axis=0)
        second = second_factor(
            summed[:, :unit_count],
            summed[:, unit_count : 2 * unit_count],
            summed[:, 2 * unit_count : 3 * unit_count],
            summed[:, 3 * unit_count :],
        )
        piece = lax.dot_general(
            normed_c,
            lax.all_gather(second, "tensor", axis=0, tiled=True),
            (((0,), (0,)), ((), ())),
            preferred_element_type=jnp.float32,
        )
        total = piece if total is None else total + piece
    return total / total_tokens


def solution(mesh):
    return jax.shard_map(
        body,
        mesh=mesh,
        in_specs=(
            P("seq", "tensor"),
            P("seq", "tensor"),
            P("tensor"),
            P("tensor", "seq"),
            P("tensor", "seq"),
            P("seq", "tensor"),
            P("tensor", "seq"),
        ),
        out_specs=P("tensor", "seq"),
        check_vma=False,
    )
```

time: 514 us -> 407 us (0.79)
  waiting for transfers between devices: 425 us -> 292 us
  matrix products: 45.3 us -> 13.8 us
  Pallas kernels: 0 us -> 30.6 us
  starting transfers between devices: 0.43 us -> 11.6 us
  local copies, waits for them, and re-layouts: 0.01 us -> 8.42 us
  other arithmetic: 5.65 us -> 12.7 us
    reduce_scatter x4 -> x0, waiting for transfers between devices: 314 us -> none  [body(): lax.psum_scatter(p, 'tensor', scatter_dimension=0, tiled=True)]
    all_to_all x0 -> x2, waiting for transfers between devices: none -> 112 us  [body(): received = lax.all_to_all(parts, 'tensor', 0, 0, tiled=True)]
    all_gather x2 -> x4, waiting for transfers between devices: 44.5 us -> 113 us  [the longest x2 72.7 us: body(): cot_c = lax.all_gather(cotangent[rows], 'seq', axis=0, tiled=True)]
    dot_general x5 -> x2, matrix products: 45.3 us -> 13.8 us  [body(): lax.dot_general(normed_c, lax.all_gather(second, 'tensor', axis=0, tiled=...]
    pallas_call x0 -> x2, Pallas kernels: none -> 30.6 us  [products(): pl.pallas_call(products_kernel, out_shape=jax.ShapeDtypeStruct((blocks, t...]
    all_to_all x0 -> x2, starting transfers between devices: none -> 11.4 us  [body(): received = lax.all_to_all(parts, 'tensor', 0, 0, tiled=True)]
    reduce_sum x0 -> x2, other arithmetic: none -> 8.54 us  [body(): summed = jnp.sum(received.astype(jnp.float32), axis=0)]
    unnamed x2 -> x10, local copies, waits for them, and re-layouts: 0.01 us -> 6 us
  transfers between devices with their start and end apart: 7 -> 8, of which waited for: 7 -> 8; matrix products, arithmetic and copies ran while one was open for 7% -> 5% of each run, Pallas kernels for 0% -> 8%
where the time goes in v2:
time: 407 us
  waiting for transfers between devices  292 us (72%)
  Pallas kernels  30.6 us (8%)
  blocking collectives  24.6 us (6%)
  matrix products  13.8 us (3%)
  between operations  13.5 us (3%)
  other arithmetic  12.7 us (3%)
  starting transfers between devices  11.6 us (3%)
  local copies, waits for them, and re-layouts  8.42 us (2%)
    all_to_all x2, waiting for transfers between devices, body(): received = lax.all_to_all(parts, 'tensor', 0, 0, tiled=True)  112 us
    all_gather x2, waiting for transfers between devices, body(): cot_c = lax.all_gather(cotangent[rows], 'seq', axis=0, tiled=True)  72.7 us
    all_gather x2, waiting for transfers between devices, body(): lax.all_gather(second, 'tensor', axis=0, tiled=True)  65.1 us
    all_gather x2, waiting for transfers between devices, body(): normed_c = lax.all_gather(normed_local[rows], 'seq', axis=0, tiled=True)  40.5 us
    pallas_call x2, Pallas kernels, products(): pl.pallas_call(products_kernel, out_shape=jax.ShapeDtypeStruct((blocks, t...  30.6 us
    psum x1, blocking collectives, body(): squares = lax.psum(jnp.sum(values * values, axis=1), 'tensor')  24.6 us
    dot_general x2, matrix products, body(): lax.dot_general(normed_c, lax.all_gather(second, 'tensor', axis=0, tiled=...  13.8 us
    all_to_all x2, starting transfers between devices, body(): received = lax.all_to_all(parts, 'tensor', 0, 0, tiled=True)  11.4 us
  transfers between devices with their start and end apart: 8, of which 8 were waited for; matrix products, arithmetic and copies ran while one was open for 5% of the time, Pallas kernels for 8%

profile of v2, /device:TPU:0, one launch (start us, length us, event | category | flops | bytes accessed | tf_op | source)
XLA Modules:
  0.0 406.8 jit_solution(1402160724851487681)
XLA Ops:
  6.5 0.0 copy-start
  6.5 0.0 all-gather.7.cloned.1.call-start
  6.5 1.2 fusion
  7.8 24.6 %psum.7 = f32[128]{0:T(128)S(1)} all-reduce(f32[128]{0:T(128)S(1)} %fusion), channel_id=1, replica_groups=mesh['seq'=16,'tensor'=8] {'tensor'}, use_global_device_ids=true, to_apply=%region_1.0 | all-reduce | flops 128 | bytes 1024 | tf_op jit(solution)/shard_map/psum | solution.py:64
  32.4 1.1 fusion.2
  33.5 0.7 fusion.12
  34.2 0.0 all-gather.7.cloned.1.call-update
  34.2 0.0 all-gather.9.cloned.1.call-start
  34.3 1.7 fusion.11
  36.0 0.0 all-gather.9.cloned.1.call-update
  36.0 0.0 all-gather.13.cloned.1.call-start
  36.0 0.7 all-gather.13.cloned.1.call-update
  36.7 28.9 %all-gather.7.cloned.1.call-done.n_ref = bf16[1024,1024]{1,0:T(8,128)(2,1)} async-done(((bf16[64,1024]{1,0:T(8,128)(2,1)}), bf16[1024,1024]{1,0:T(8,128)(2,1)}) %all-gather.7.cloned.1.call-update) | async-done | bytes 2097168 | tf_op jit(solution)/shard_map/all_gather | solution.py:75
  65.7 35.6 %all-gather.9.cloned.1.call-done.c_ref = bf16[1024,1024]{1,0:T(8,128)(2,1)} async-done(((bf16[64,1024]{1,0:T(8,128)(2,1)}), bf16[1024,1024]{1,0:T(8,128)(2,1)}) %all-gather.9.cloned.1.call-update) | async-done | bytes 2097168 | tf_op jit(solution)/shard_map/all_gather | solution.py:74
  101.3 0.0 copy-done
  101.3 0.0 copy-start.1
  101.3 1.5 copy-done.1
  102.8 0.0 copy-start.3
  102.8 1.5 copy-done.3
  104.3 15.3 %shard_map.73 = bf16[8,128,3584]{2,1,0:T(8,128)(2,1)} custom-call(bf16[1024,1024]{1,0:T(8,128)(2,1)} %all-gather.7.cloned.1.call-done.n_ref, bf16[1024,1024]{1,0:T(8,128)(2,1)} %all-gather.9.cloned.1.call-done.c_ref, bf16[1024,896]{1,0:T(8,128)(2,1)S(1)} %copy-done, bf16[1024,896]{1,0:T(8,128)(2,1)S(1)} %copy-done.1, bf16[1024,896]{1,0:T(8,128)(2,1)S(1)} %copy-done.3, ...), custom_call_target="tpu_custom_call" | custom-call | flops 7516192768 | bytes 18874368 | tf_op jit(solution)/shard_map/pallas_call | solution.py:39
  119.6 6.5 %all-to-all-start = ((bf16[8,128,3584]{2,1,0:T(8,128)(2,1)}), bf16[8,128,3584]{2,1,0:T(8,128)(2,1)}, u32[]{:S(2)}, u32[]{:S(2)}) async-start(bf16[8,128,3584]{2,1,0:T(8,128)(2,1)} %shard_map.73), calls=%async_computation | async-start | bytes 14680064 | tf_op jit(solution)/shard_map/all_to_all | solution.py:78
  126.1 0.0 all-gather.15.cloned.1.call-start
  126.1 0.5 all-gather.15.cloned.1.call-update
  126.6 11.5 %all-gather.13.cloned.1.call-done.n_ref = bf16[1024,1024]{1,0:T(8,128)(2,1)} async-done(((bf16[64,1024]{1,0:T(8,128)(2,1)}), bf16[1024,1024]{1,0:T(8,128)(2,1)}) %all-gather.13.cloned.1.call-update) | async-done | bytes 2097168 | tf_op jit(solution)/shard_map/all_gather | solution.py:75
  138.2 37.0 %all-gather.15.cloned.1.call-done.c_ref = bf16[1024,1024]{1,0:T(8,128)(2,1)} async-done(((bf16[64,1024]{1,0:T(8,128)(2,1)}), bf16[1024,1024]{1,0:T(8,128)(2,1)}) %all-gather.15.cloned.1.call-update) | async-done | bytes 2097168 | tf_op jit(solution)/shard_map/all_gather | solution.py:74
  175.2 0.0 copy-start.2
  175.2 1.5 copy-done.2
  176.7 0.0 copy-start.4
  176.7 1.5 copy-done.4
  178.2 15.3 %shard_map.74 = bf16[8,128,3584]{2,1,0:T(8,128)(2,1)} custom-call(bf16[1024,1024]{1,0:T(8,128)(2,1)} %all-gather.13.cloned.1.call-done.n_ref, bf16[1024,1024]{1,0:T(8,128)(2,1)} %all-gather.15.cloned.1.call-done.c_ref, bf16[1024,896]{1,0:T(8,128)(2,1)S(1)} %copy-done, bf16[1024,896]{1,0:T(8,128)(2,1)S(1)} %copy-done.2, bf16[1024,896]{1,0:T(8,128)(2,1)S(1)} %copy-done.4, ...), custom_call_target="tpu_custom_call" | custom-call | flops 7516192768 | bytes 18874368 | tf_op jit(solution)/shard_map/pallas_call | solution.py:39
  193.6 30.1 %all-to-all-done = bf16[8,128,3584]{2,1,0:T(8,128)(2,1)} async-done(((bf16[8,128,3584]{2,1,0:T(8,128)(2,1)}), bf16[8,128,3584]{2,1,0:T(8,128)(2,1)}, u32[]{:S(2)}, u32[]{:S(2)}) %all-to-all-start) | async-done | bytes 7340064 | tf_op jit(solution)/shard_map/all_to_all | solution.py:78
  223.6 4.9 %all-to-all-start.1 = ((bf16[8,128,3584]{2,1,0:T(8,128)(2,1)}), bf16[8,128,3584]{2,1,0:T(8,128)(2,1)}, u32[]{:S(2)}, u32[]{:S(2)}) async-start(bf16[8,128,3584]{2,1,0:T(8,128)(2,1)} %shard_map.74), calls=%async_computation.1 | async-start | bytes 14680064 | tf_op jit(solution)/shard_map/all_to_all | solution.py:78
  228.5 0.0 all-gather.11.cloned.1.call-start
  228.6 4.3 %convert_reduce_fusion.1 = f32[128,3584]{1,0:T(8,128)S(1)} fusion(bf16[8,128,3584]{2,1,0:T(8,128)(2,1)} %all-to-all-done), kind=kLoop, calls=%fused_computation.1 | loop fusion | flops 6881280 | bytes 9175040 | tf_op jit(solution)/shard_map/reduce_sum | solution.py:79
  232.8 0.9 fusion.6
  233.8 0.0 all-gather.11.cloned.1.call-update
  233.8 0.0 all-gather.17.cloned.1.call-start
  233.8 82.0 %all-to-all-done.1 = bf16[8,128,3584]{2,1,0:T(8,128)(2,1)} async-done(((bf16[8,128,3584]{2,1,0:T(8,128)(2,1)}), bf16[8,128,3584]{2,1,0:T(8,128)(2,1)}, u32[]{:S(2)}, u32[]{:S(2)}) %all-to-all-start.1) | async-done | bytes 7340064 | tf_op jit(solution)/shard_map/all_to_all | solution.py:78
  315.8 4.3 %convert_reduce_fusion = f32[128,3584]{1,0:T(8,128)S(1)} fusion(bf16[8,128,3584]{2,1,0:T(8,128)(2,1)} %all-to-all-done.1), kind=kLoop, calls=%fused_computation | loop fusion | flops 6881280 | bytes 9175040 | tf_op jit(solution)/shard_map/reduce_sum | solution.py:79
  320.1 0.9 fusion.10
  321.0 0.0 all-gather.17.cloned.1.call-update
  321.0 19.6 %all-gather.11.cloned.1.call-done = bf16[1024,896]{1,0:T(8,128)(2,1)} async-done(((bf16[128,896]{1,0:T(8,128)(2,1)}), bf16[1024,896]{1,0:T(8,128)(2,1)}) %all-gather.11.cloned.1.call-update) | async-done | bytes 1835024 | tf_op jit(solution)/shard_map/all_gather | solution.py:88
  340.7 6.3 %fusion.13 = f32[1024,896]{1,0:T(8,128)} fusion(bf16[1024,1024]{1,0:T(8,128)(2,1)} %all-gather.7.cloned.1.call-done.n_ref, bf16[1024,896]{1,0:T(8,128)(2,1)} %all-gather.11.cloned.1.call-done), kind=kOutput, calls=%fused_computation.23 | convolution fusion | flops 1879048192 | bytes 7602176 | tf_op jit(solution)/shard_map/dot_general | solution.py:86
  347.0 45.5 %all-gather.17.cloned.1.call-done = bf16[1024,896]{1,0:T(8,128)(2,1)} async-done(((bf16[128,896]{1,0:T(8,128)(2,1)}), bf16[1024,896]{1,0:T(8,128)(2,1)}) %all-gather.17.cloned.1.call-update) | async-done | bytes 1835024 | tf_op jit(solution)/shard_map/all_gather | solution.py:88
  392.5 7.5 %add_multiply_fusion = f32[1024,896]{1,0:T(8,128)} fusion(f32[1024,896]{1,0:T(8,128)} %fusion.13, bf16[1024,1024]{1,0:T(8,128)(2,1)} %all-gather.13.cloned.1.call-done.n_ref, bf16[1024,896]{1,0:T(8,128)(2,1)} %all-gather.17.cloned.1.call-done), kind=kOutput, calls=%fused_computation.2 | convolution fusion | flops 1880883200 | bytes 11272192 | tf_op jit(solution)/shard_map/dot_general | solution.py:86
  (1 shorter events, 0.0 us)
Async XLA Ops:
  6.5 94.8 %copy-start = (bf16[1024,896]{1,0:T(8,128)(2,1)S(1)}, bf16[1024,896]{1,0:T(8,128)(2,1)}, u32[]{:S(2)}) copy-start(bf16[1024,896]{1,0:T(8,128)(2,1)} %wg_ref.3) | copy-start | bytes 5505028
  6.5 59.1 %all-gather.7.cloned.1.call-start = ((), (), s32[]{:S(2)}) async-start(), calls=%async_computation.2 | async-start | bytes 2228224 | tf_op jit(solution)/shard_map/all_gather | solution.py:75
  34.2 67.1 %all-gather.9.cloned.1.call-start = ((), (), s32[]{:S(2)}) async-start(), calls=%async_computation.3 | async-start | bytes 2228224 | tf_op jit(solution)/shard_map/all_gather | solution.py:74
  36.0 102.2 %all-gather.13.cloned.1.call-start = ((), (), s32[]{:S(2)}) async-start(), calls=%async_computation.5 | async-start | bytes 2228224 | tf_op jit(solution)/shard_map/all_gather | solution.py:75
  101.3 1.5 copy-start.1
  102.8 1.5 copy-start.3
  119.6 104.0 %all-to-all-start = ((bf16[8,128,3584]{2,1,0:T(8,128)(2,1)}), bf16[8,128,3584]{2,1,0:T(8,128)(2,1)}, u32[]{:S(2)}, u32[]{:S(2)}) async-start(bf16[8,128,3584]{2,1,0:T(8,128)(2,1)} %shard_map.73), calls=%async_computation | async-start | bytes 14680064 | tf_op jit(solution)/shard_map/all_to_all | solution.py:78
  126.1 49.2 %all-gather.15.cloned.1.call-start = ((), (), s32[]{:S(2)}) async-start(), calls=%async_computation.6 | async-start | bytes 2228224 | tf_op jit(solution)/shard_map/all_gather | solution.py:74
  175.2 1.5 copy-start.2
  176.7 1.5 copy-start.4
  223.6 92.2 %all-to-all-start.1 = ((bf16[8,128,3584]{2,1,0:T(8,128)(2,1)}), bf16[8,128,3584]{2,1,0:T(8,128)(2,1)}, u32[]{:S(2)}, u32[]{:S(2)}) async-start(bf16[8,128,3584]{2,1,0:T(8,128)(2,1)} %shard_map.74), calls=%async_computation.1 | async-start | bytes 14680064 | tf_op jit(solution)/shard_map/all_to_all | solution.py:78
  228.5 112.1 %all-gather.11.cloned.1.call-start = ((), (), s32[]{:S(2)}) async-start(), calls=%async_computation.4 | async-start | bytes 2064384 | tf_op jit(solution)/shard_map/all_gather | solution.py:88
  233.8 158.7 %all-gather.17.cloned.1.call-start = ((), (), s32[]{:S(2)}) async-start(), calls=%async_computation.7 | async-start | bytes 2064384 | tf_op jit(solution)/shard_map/all_gather | solution.py:88
Sparse Core Ops, SparseCore 0:
  34.3 31.2 all-gather.6
  67.4 33.8 all-gather.8
  103.0 35.1 all-gather.12
  139.7 35.4 all-gather.14
  233.9 106.7 all-gather.10
  342.8 49.6 all-gather.16

commit v3 on v2

--- a/solution.py
+++ b/solution.py
@@ -8,7 +8,6 @@
 from jax.sharding import PartitionSpec as P
 
 D = 8192
-CHUNKS = 2
 
 epsilon = 1e-05
 
@@ -58,39 +57,42 @@
     )(normed, cot, w_gate, w_up, probe, w_down)
 
 
+def butterfly_sum(x, axis):
+    n = lax.axis_size(axis)
+    bit = 1
+    while bit < n:
+        x = x + lax.ppermute(x, axis, [(i, i ^ bit) for i in range(n)])
+        bit *= 2
+    return x
+
+
 def body(tokens, cotangent, gain, w_gate, w_up, w_down, probe):
     n_tensor = lax.axis_size("tensor")
-    values = tokens.astype(jnp.float32)
-    squares = lax.psum(jnp.sum(values * values, axis=1), "tensor")
+    width = tokens.shape[1]
+    both = lax.all_gather(jnp.concatenate([tokens, cotangent], axis=1), "seq", axis=0, tiled=True)
+    gathered = both[:, :width]
+    upstream_rows = both[:, width:]
+    values = gathered.astype(jnp.float32)
+    squares = butterfly_sum(jnp.sum(values * values, axis=1), "tensor")
     inverse = lax.rsqrt(squares / D + epsilon)
-    normed_local = (values * inverse[:, None] * gain[None, :]).astype(jnp.bfloat16)
-    local_rows = tokens.shape[0]
-    step = local_rows // CHUNKS
+    normed = (values * inverse[:, None] * gain[None, :]).astype(jnp.bfloat16)
+    total_tokens = normed.shape[0]
     unit_count = w_gate.shape[1]
-    total = None
-    total_tokens = 0
-    for c in range(CHUNKS):
-        rows = slice(c * step, (c + 1) * step)
-        cot_c = lax.all_gather(cotangent[rows], "seq", axis=0, tiled=True)
-        normed_c = lax.all_gather(normed_local[rows], "seq", axis=0, tiled=True)
-        total_tokens += normed_c.shape[0]
-        parts = products(normed_c, cot_c, w_gate, w_up, probe, w_down, n_tensor)
-        received = lax.all_to_all(parts, "tensor", 0, 0, tiled=True)
-        summed = jnp.sum(received.astype(jnp.float32), axis=0)
-        second = second_factor(
-            summed[:, :unit_count],
-            summed[:, unit_count : 2 * unit_count],
-            summed[:, 2 * unit_count : 3 * unit_count],
-            summed[:, 3 * unit_count :],
-        )
-        piece = lax.dot_general(
-            normed_c,
-            lax.all_gather(second, "tensor", axis=0, tiled=True),
-            (((0,), (0,)), ((), ())),
-            preferred_element_type=jnp.float32,
-        )
-        total = piece if total is None else total + piece
-    return total / total_tokens
+    parts = products(normed, upstream_rows, w_gate, w_up, probe, w_down, n_tensor)
+    summed = lax.psum_scatter(parts, "tensor", scatter_dimension=0, tiled=True)[0].astype(jnp.float32)
+    second = second_factor(
+        summed[:, :unit_count],
+        summed[:, unit_count : 2 * unit_count],
+        summed[:, 2 * unit_count : 3 * unit_count],
+        summed[:, 3 * unit_count :],
+    )
+    product = lax.dot_general(
+        normed,
+        lax.all_gather(second, "tensor", axis=0, tiled=True),
+        (((0,), (0,)), ((), ())),
+        preferred_element_type=jnp.float32,
+    )
+    return product / total_tokens
 
 
 def solution(mesh):

time: 407 us -> 363 us (0.89)
  blocking collectives: 24.6 us -> 0 us
  Pallas kernels: 30.6 us -> 22 us
  matrix products: 13.8 us -> 9.71 us
    reduce_scatter x0 -> x1, waiting for transfers between devices: none -> 169 us  [body(): lax.psum_scatter(parts, 'tensor', scatter_dimension=0, tiled=True)[0]]
    all_to_all x2 -> x0, waiting for transfers between devices: 112 us -> none  [body(): received = lax.all_to_all(parts, 'tensor', 0, 0, tiled=True)]
    all_gather x4 -> x1, waiting for transfers between devices: 113 us -> 55.2 us  [body(): lax.all_gather(jnp.concatenate([tokens, cotangent], axis=1), 'seq', axis=...]
    psum x1 -> x0, blocking collectives: 24.6 us -> none  [body(): squares = lax.psum(jnp.sum(values * values, axis=1), 'tensor')]
    all_to_all x2 -> x0, starting transfers between devices: 11.4 us -> none  [body(): received = lax.all_to_all(parts, 'tensor', 0, 0, tiled=True)]
    pallas_call x2 -> x1, Pallas kernels: 30.6 us -> 22 us  [products(): pl.pallas_call(products_kernel, out_shape=jax.ShapeDtypeStruct((blocks, t...]
    ppermute x0 -> x3, starting transfers between devices: none -> 7.63 us  [butterfly_sum(): x = x + lax.ppermute(x, axis, [(i, i ^ bit) for i in range(n)])]
    reduce_sum x3 -> x1, other arithmetic: 9.75 us -> 3.07 us  [body(): squares = butterfly_sum(jnp.sum(values * values, axis=1), 'tensor')]
  transfers between devices with their start and end apart: 8 -> 6, of which waited for: 8 -> 5; matrix products, arithmetic and copies ran while one was open for 5% -> 1% of each run, Pallas kernels for 8% -> 0%
where the time goes in v3:
time: 363 us
  waiting for transfers between devices  293 us (81%)
  Pallas kernels  22 us (6%)
  between operations  13.2 us (4%)
  other arithmetic  10.8 us (3%)
  matrix products  9.71 us (3%)
  starting transfers between devices  7.72 us (2%)
  local copies, waits for them, and re-layouts  6.06 us (2%)
    reduce_scatter x1, waiting for transfers between devices, body(): lax.psum_scatter(parts, 'tensor', scatter_dimension=0, tiled=True)[0]  169 us
    all_gather x1, waiting for transfers between devices, body(): lax.all_gather(second, 'tensor', axis=0, tiled=True)  64.7 us
    all_gather x1, waiting for transfers between devices, body(): lax.all_gather(jnp.concatenate([tokens, cotangent], axis=1), 'seq', axis=...  55.2 us
    pallas_call x1, Pallas kernels, products(): pl.pallas_call(products_kernel, out_shape=jax.ShapeDtypeStruct((blocks, t...  22 us
    dot_general x1, matrix products, body(): lax.dot_general(normed, lax.all_gather(second, 'tensor', axis=0, tiled=Tr...  9.71 us
    ppermute x3, starting transfers between devices, butterfly_sum(): x = x + lax.ppermute(x, axis, [(i, i ^ bit) for i in range(n)])  7.63 us
  transfers between devices with their start and end apart: 6, of which 5 were waited for; matrix products, arithmetic and copies ran while one was open for 1% of the time, Pallas kernels for 0%

profile of v3, /device:TPU:0, one launch (start us, length us, event | category | flops | bytes accessed | tf_op | source)
XLA Modules:
  0.0 362.7 jit_solution(8668995179078781138)
XLA Ops:
  6.5 0.0 all-gather.3.cloned.1.call-start
  6.5 1.9 pad_maximum_fusion
  8.4 0.0 all-gather.3.cloned.1.call-update
  8.4 0.0 reduce-scatter.2.cloned.1.call-start
  8.5 55.2 %all-gather.3.cloned.1.call-done = bf16[2048,2048]{1,0:T(8,128)(2,1)} async-done(((bf16[128,2048]{1,0:T(8,128)(2,1)}), bf16[2048,2048]{1,0:T(8,128)(2,1)}) %all-gather.3.cloned.1.call-update) | async-done | bytes 8388624 | tf_op jit(solution)/shard_map/all_gather | solution.py:72
  63.7 3.1 fusion
  66.7 3.1 collective-permute-start
  69.8 2.2 collective-permute-done
  72.0 1.5 collective-permute-start.1
  73.5 2.2 collective-permute-done.1
  75.6 0.0 copy-start.3
  75.6 0.0 copy-start.4
  75.6 3.1 collective-permute-start.2
  78.7 4.7 %slice.25.c_ref = bf16[2048,1024]{1,0:T(8,128)(2,1)} slice(bf16[2048,2048]{1,0:T(8,128)(2,1)} %all-gather.3.cloned.1.call-done), slice={[0:2048], [1024:2048]} | slice | bytes 8388608 | tf_op jit(solution)/shard_map/slice | solution.py:74
  83.4 0.0 collective-permute-done.2
  83.4 0.0 copy-done.3
  83.4 0.0 copy-done.4
  83.4 0.0 copy-start
  83.4 0.0 copy-start.1
  83.4 0.0 copy-start.2
  83.4 2.7 fusion.2.n_ref
  86.1 0.0 copy-done
  86.1 0.5 copy-done.1
  86.7 0.9 copy-done.2
  87.5 22.0 %shard_map.73 = bf16[8,256,3584]{2,1,0:T(8,128)(2,1)} custom-call(bf16[2048,1024]{1,0:T(8,128)(2,1)} %fusion.2.n_ref, bf16[2048,1024]{1,0:T(8,128)(2,1)} %slice.25.c_ref, bf16[1024,896]{1,0:T(8,128)(2,1)S(1)} %copy-done, bf16[1024,896]{1,0:T(8,128)(2,1)S(1)} %copy-done.1, bf16[1024,896]{1,0:T(8,128)(2,1)S(1)} %copy-done.2, bf16[896,1024]{1,0:T(8,128)(2,1)} %wd_ref.1), custom_call_target="tpu_custom_call" | custom-call | flops 15032385536 | bytes 30408704 | tf_op jit(solution)/shard_map/pallas_call | solution.py:38
  109.5 0.0 reduce-scatter.2.cloned.1.call-update
  109.5 0.0 all-gather.5.cloned.1.call-start
  109.6 169.0 %reduce-scatter.2.cloned.1.call-done = bf16[1,256,3584]{2,1,0:T(8,128)(2,1)} async-done(((bf16[8,256,3584]{2,1,0:T(8,128)(2,1)}), bf16[1,256,3584]{2,1,0:T(8,128)(2,1)}) %reduce-scatter.2.cloned.1.call-update) | async-done | bytes 1835024 | tf_op jit(solution)/shard_map/reduce_scatter | solution.py:82
  278.6 1.9 bitcast_convert_fusion
  280.5 1.2 fusion.6
  281.8 0.0 all-gather.5.cloned.1.call-update
  281.8 64.7 %all-gather.5.cloned.1.call-done = bf16[2048,896]{1,0:T(8,128)(2,1)} async-done(((bf16[256,896]{1,0:T(8,128)(2,1)}), bf16[2048,896]{1,0:T(8,128)(2,1)}) %all-gather.5.cloned.1.call-update) | async-done | bytes 3670032 | tf_op jit(solution)/shard_map/all_gather | solution.py:91
  346.5 9.7 %convolution_multiply_fusion = f32[1024,896]{1,0:T(8,128)} fusion(bf16[2048,1024]{1,0:T(8,128)(2,1)} %fusion.2.n_ref, bf16[2048,896]{1,0:T(8,128)(2,1)} %all-gather.5.cloned.1.call-done), kind=kOutput, calls=%fused_computation.5 | convolution fusion | flops 3759013888 | bytes 11534336 | tf_op jit(solution)/shard_map/dot_general | solution.py:89
  (3 shorter events, 0.0 us)
Async XLA Ops:
  6.5 57.1 %all-gather.3.cloned.1.call-start = ((), (), s32[]{:S(2)}) async-start(), calls=%async_computation.1 | async-start | bytes 8912896 | tf_op jit(solution)/shard_map/all_gather | solution.py:72
  8.4 270.2 %reduce-scatter.2.cloned.1.call-start = ((), (), s32[]{:S(2)}) async-start(), calls=%async_computation.2 | async-start | bytes 16515072 | tf_op jit(solution)/shard_map/reduce_scatter | solution.py:82
  66.7 5.2 %collective-permute-start = (f32[2048]{0:T(1024)S(1)}, f32[2048]{0:T(1024)S(1)}, u32[]{:S(2)}, u32[]{:S(2)}) collective-permute-start(f32[2048]{0:T(1024)S(1)} %fusion), channel_id=1, source_target_pairs={{0,1},{1,0},{2,3},{3,2},{4,5},{5,4},{6,7},{7,6},{8,9},{9,8},{10,11... | collective-permute-start | bytes 24584 | tf_op jit(solution)/shard_map/ppermute | solution.py:64
  72.0 3.7 %collective-permute-start.1 = (f32[2048]{0:T(1024)S(1)}, f32[2048]{0:T(1024)S(1)}, u32[]{:S(2)}, u32[]{:S(2)}) collective-permute-start(f32[2048]{0:T(1024)S(1)} %add.23), channel_id=1, source_target_pairs={{0,2},{1,3},{2,0},{3,1},{4,6},{5,7},{6,4},{7,5},{8,10},{9,11},{10,... | collective-permute-start | bytes 24584 | tf_op jit(solution)/shard_map/ppermute | solution.py:64
  75.6 7.8 %copy-start.3 = (bf16[2048,2048]{1,0:T(8,128)(2,1)S(1)}, bf16[2048,2048]{1,0:T(8,128)(2,1)}, u32[]{:S(2)}) copy-start(bf16[2048,2048]{1,0:T(8,128)(2,1)} %all-gather.3.cloned.1.call-done) | copy-start | bytes 25165828
  75.6 7.8 %copy-start.4 = (f32[1024]{0:T(1024)S(1)}, f32[1024]{0:T(1024)}, u32[]{:S(2)}) copy-start(f32[1024]{0:T(1024)} %param.9) | copy-start | bytes 12292
  75.6 7.7 %collective-permute-start.2 = (f32[2048]{0:T(1024)S(1)}, f32[2048]{0:T(1024)S(1)}, u32[]{:S(2)}, u32[]{:S(2)}) collective-permute-start(f32[2048]{0:T(1024)S(1)} %add.24), channel_id=1, source_target_pairs={{0,4},{1,5},{2,6},{3,7},{4,0},{5,1},{6,2},{7,3},{8,12},{9,13},{10,... | collective-permute-start | bytes 24584 | tf_op jit(solution)/shard_map/ppermute | solution.py:64
  83.4 2.7 copy-start
  83.4 3.3 copy-start.1
  83.4 4.1 %copy-start.2 = (bf16[1024,896]{1,0:T(8,128)(2,1)S(1)}, bf16[1024,896]{1,0:T(8,128)(2,1)}, u32[]{:S(2)}) copy-start(bf16[1024,896]{1,0:T(8,128)(2,1)} %pr_ref.1) | copy-start | bytes 5505028
  109.5 236.9 %all-gather.5.cloned.1.call-start = ((), (), s32[]{:S(2)}) async-start(), calls=%async_computation.3 | async-start | bytes 4128768 | tf_op jit(solution)/shard_map/all_gather | solution.py:91
Sparse Core Ops, SparseCore 0:
  9.0 54.5 all-gather.2
  109.7 168.8 reduce-scatter.1
  281.9 64.5 all-gather.4

commit v4 on v3

--- a/solution.py
+++ b/solution.py
@@ -30,8 +30,8 @@
     ).astype(o_ref.dtype)
 
 
-def products(normed, cot, w_gate, w_up, probe, w_down, blocks):
-    rows, width = normed.shape
+def products(both, w_gate, w_up, probe, w_down, blocks):
+    rows, width = both.shape[0], both.shape[1] // 2
     f = w_gate.shape[1]
     tm = rows // blocks
     full = lambda shape: pl.BlockSpec(shape, lambda i: (0, 0))
@@ -41,7 +41,7 @@
         grid=(blocks,),
         in_specs=[
             pl.BlockSpec((tm, width), lambda i: (i, 0)),
-            pl.BlockSpec((tm, width), lambda i: (i, 0)),
+            pl.BlockSpec((tm, width), lambda i: (i, 1)),
             full(w_gate.shape),
             full(w_up.shape),
             full(probe.shape),
@@ -54,7 +54,14 @@
             transcendentals=0,
             bytes_accessed=2 * (2 * rows * width + 4 * width * f + rows * 4 * f),
         ),
-    )(normed, cot, w_gate, w_up, probe, w_down)
+    )(both, both, w_gate, w_up, probe, w_down)
+
+
+def gather_tensor(x, axis):
+    n = lax.axis_size(axis)
+    repeated = jnp.broadcast_to(x[None], (n,) + x.shape)
+    got = lax.all_to_all(repeated, axis, 0, 0, tiled=True)
+    return got.reshape((n * x.shape[0],) + x.shape[1:])
 
 
 def butterfly_sum(x, axis):
@@ -69,16 +76,14 @@
 def body(tokens, cotangent, gain, w_gate, w_up, w_down, probe):
     n_tensor = lax.axis_size("tensor")
     width = tokens.shape[1]
-    both = lax.all_gather(jnp.concatenate([tokens, cotangent], axis=1), "seq", axis=0, tiled=True)
-    gathered = both[:, :width]
-    upstream_rows = both[:, width:]
-    values = gathered.astype(jnp.float32)
+    values = tokens.astype(jnp.float32)
     squares = butterfly_sum(jnp.sum(values * values, axis=1), "tensor")
     inverse = lax.rsqrt(squares / D + epsilon)
-    normed = (values * inverse[:, None] * gain[None, :]).astype(jnp.bfloat16)
-    total_tokens = normed.shape[0]
+    normed_local = (values * inverse[:, None] * gain[None, :]).astype(jnp.bfloat16)
+    both = lax.all_gather(jnp.concatenate([normed_local, cotangent], axis=1), "seq", axis=0, tiled=True)
+    total_tokens = both.shape[0]
     unit_count = w_gate.shape[1]
-    parts = products(normed, upstream_rows, w_gate, w_up, probe, w_down, n_tensor)
+    parts = products(both, w_gate, w_up, probe, w_down, n_tensor)
     summed = lax.psum_scatter(parts, "tensor", scatter_dimension=0, tiled=True)[0].astype(jnp.float32)
     second = second_factor(
         summed[:, :unit_count],
@@ -87,8 +92,8 @@
         summed[:, 3 * unit_count :],
     )
     product = lax.dot_general(
-        normed,
-        lax.all_gather(second, "tensor", axis=0, tiled=True),
+        both[:, :width],
+        gather_tensor(second, "tensor"),
         (((0,), (0,)), ((), ())),
         preferred_element_type=jnp.float32,
     )

time: 363 us -> 340 us (0.937)
  waiting for transfers between devices: 293 us -> 231 us
  blocking collectives: 0 us -> 47.6 us
  other arithmetic: 10.8 us -> 6.37 us
    all_gather x2 -> x1, waiting for transfers between devices: 120 us -> 54.7 us  [body(): lax.all_gather(jnp.concatenate([normed_local, cotangent], axis=1), 'seq',...]
    all_to_all x0 -> x1, blocking collectives: none -> 47.6 us  [gather_tensor(): got = lax.all_to_all(repeated, axis, 0, 0, tiled=True)]
    slice x1 -> x0, local copies, waits for them, and re-layouts: 4.65 us -> none  [body(): upstream_rows = both[:, width:]]
  transfers between devices with their start and end apart: 6 -> 5, of which waited for: 5 -> 5; matrix products, arithmetic and copies ran while one was open for 1% -> 0% of each run, Pallas kernels for 0% -> 0%
where the time goes in v4:
time: 340 us
  waiting for transfers between devices  231 us (68%)
  blocking collectives  47.6 us (14%)
  Pallas kernels  22.2 us (7%)
  between operations  13.5 us (4%)
  starting transfers between devices  8.25 us (2%)
  matrix products  6.4 us (2%)
  other arithmetic  6.37 us (2%)
  local copies, waits for them, and re-layouts  4.98 us (1%)
    reduce_scatter x1, waiting for transfers between devices, body(): lax.psum_scatter(parts, 'tensor', scatter_dimension=0, tiled=True)[0]  170 us
    all_gather x1, waiting for transfers between devices, body(): lax.all_gather(jnp.concatenate([normed_local, cotangent], axis=1), 'seq',...  54.7 us
    all_to_all x1, blocking collectives, gather_tensor(): got = lax.all_to_all(repeated, axis, 0, 0, tiled=True)  47.6 us
    pallas_call x1, Pallas kernels, products(): pl.pallas_call(products_kernel, out_shape=jax.ShapeDtypeStruct((blocks, t...  22.2 us
    ppermute x3, starting transfers between devices, butterfly_sum(): x = x + lax.ppermute(x, axis, [(i, i ^ bit) for i in range(n)])  8.2 us
  transfers between devices with their start and end apart: 5, of which 5 were waited for; matrix products, arithmetic and copies ran while one was open for 0% of the time, Pallas kernels for 0%

profile of v4, /device:TPU:0, one launch (start us, length us, event | category | flops | bytes accessed | tf_op | source)
XLA Modules:
  0.0 339.7 jit_solution(3337309557358112072)
XLA Ops:
  6.5 0.0 all-gather.2.cloned.1.call-start
  6.5 1.1 fusion.9
  7.6 3.2 collective-permute-start
  10.8 1.9 collective-permute-done
  12.8 1.7 collective-permute-start.1
  14.5 1.9 collective-permute-done.1
  16.3 3.3 collective-permute-start.2
  19.6 1.8 collective-permute-done.2
  21.4 1.1 fusion.11
  22.5 1.8 pad_maximum_fusion
  24.3 0.0 all-gather.2.cloned.1.call-update
  24.3 0.0 reduce-scatter.2.cloned.1.call-start
  24.4 54.7 %all-gather.2.cloned.1.call-done.n_ref.c_ref = bf16[2048,2048]{1,0:T(8,128)(2,1)} async-done(((bf16[128,2048]{1,0:T(8,128)(2,1)}), bf16[2048,2048]{1,0:T(8,128)(2,1)}) %all-gather.2.cloned.1.call-update) | async-done | bytes 8388624 | tf_op jit(solution)/shard_map/all_gather | solution.py:83
  79.1 0.0 copy-start
  79.1 1.5 copy-done
  80.6 0.0 copy-start.1
  80.6 1.5 copy-done.1
  82.1 0.0 copy-start.2
  82.1 1.5 copy-done.2
  83.6 22.2 %shard_map.73 = bf16[8,256,3584]{2,1,0:T(8,128)(2,1)} custom-call(bf16[2048,2048]{1,0:T(8,128)(2,1)} %all-gather.2.cloned.1.call-done.n_ref.c_ref, bf16[2048,2048]{1,0:T(8,128)(2,1)} %all-gather.2.cloned.1.call-done.n_ref.c_ref, bf16[1024,896]{1,0:T(8,128)(2,1)S(1)} %copy-done, bf16[1024,896]{1,0:T(8,128)(2,1)S(1)} %copy-done.1, ...), custom_call_target="tpu_custom_call" | custom-call | flops 15032385536 | bytes 30408704 | tf_op jit(solution)/shard_map/pallas_call | solution.py:38
  105.7 0.0 reduce-scatter.2.cloned.1.call-update
  105.7 170.2 %reduce-scatter.2.cloned.1.call-done = bf16[1,256,3584]{2,1,0:T(8,128)(2,1)} async-done(((bf16[8,256,3584]{2,1,0:T(8,128)(2,1)}), bf16[1,256,3584]{2,1,0:T(8,128)(2,1)}) %reduce-scatter.2.cloned.1.call-update) | async-done | bytes 1835024 | tf_op jit(solution)/shard_map/reduce_scatter | solution.py:87
  276.0 1.9 bitcast_convert_fusion
  277.9 0.0 slice-start
  277.9 0.5 fusion.8
  278.4 0.0 slice-start.1
  278.4 0.5 broadcast_in_dim.2
  278.9 47.6 %all_to_all.5 = bf16[8,256,896]{2,1,0:T(8,128)(2,1)S(1)} all-to-all(bf16[8,256,896]{2,1,0:T(8,128)(2,1)S(1)} %broadcast_in_dim.2), channel_id=1, replica_groups=mesh['seq'=16,'tensor'=8] {'tensor'}, dimensions={0} | all-to-all | bytes 7340032 | tf_op jit(solution)/shard_map/all_to_all | solution.py:63
  326.4 0.0 slice-done
  326.4 0.0 slice-done.1
  326.4 6.4 %fusion.2 = f32[1024,896]{1,0:T(8,128)} fusion(bf16[2048,896]{1,0:T(8,128)(2,1)S(1)} %bitcast.5, bf16[2048,2048]{1,0:T(8,128)(2,1)S(1)} %bitcast.7), kind=kOutput, calls=%fused_computation.2 | convolution fusion | flops 3759013888 | bytes 11534336 | tf_op jit(solution)/shard_map/dot_general | solution.py:94
  (4 shorter events, 0.0 us)
Async XLA Ops:
  6.5 72.5 %all-gather.2.cloned.1.call-start = ((), (), s32[]{:S(2)}) async-start(), calls=%async_computation.2 | async-start | bytes 8912896 | tf_op jit(solution)/shard_map/all_gather | solution.py:83
  7.6 5.1 %collective-permute-start = (f32[128]{0:T(128)S(1)}, f32[128]{0:T(128)S(1)}, u32[]{:S(2)}, u32[]{:S(2)}) collective-permute-start(f32[128]{0:T(128)S(1)} %fusion.9), channel_id=1, source_target_pairs={{0,1},{1,0},{2,3},{3,2},{4,5},{5,4},{6,7},{7,6},{8,9},{9,8},{10,11... | collective-permute-start | bytes 1544 | tf_op jit(solution)/shard_map/ppermute | solution.py:71
  12.8 3.6 %collective-permute-start.1 = (f32[128]{0:T(128)S(1)}, f32[128]{0:T(128)S(1)}, u32[]{:S(2)}, u32[]{:S(2)}) collective-permute-start(f32[128]{0:T(128)S(1)} %add.23), channel_id=1, source_target_pairs={{0,2},{1,3},{2,0},{3,1},{4,6},{5,7},{6,4},{7,5},{8,10},{9,11},{10,... | collective-permute-start | bytes 1544 | tf_op jit(solution)/shard_map/ppermute | solution.py:71
  16.3 5.1 %collective-permute-start.2 = (f32[128]{0:T(128)S(1)}, f32[128]{0:T(128)S(1)}, u32[]{:S(2)}, u32[]{:S(2)}) collective-permute-start(f32[128]{0:T(128)S(1)} %add.24), channel_id=1, source_target_pairs={{0,4},{1,5},{2,6},{3,7},{4,0},{5,1},{6,2},{7,3},{8,12},{9,13},{10,... | collective-permute-start | bytes 1544 | tf_op jit(solution)/shard_map/ppermute | solution.py:71
  24.3 251.6 %reduce-scatter.2.cloned.1.call-start = ((), (), s32[]{:S(2)}) async-start(), calls=%async_computation.3 | async-start | bytes 16515072 | tf_op jit(solution)/shard_map/reduce_scatter | solution.py:87
  79.1 1.5 copy-start
  80.6 1.5 copy-start.1
  82.1 1.5 copy-start.2
  277.9 48.6 %slice-start = ((s8[8388608]{0:T(1024)(128)(4,1)}), s8[4194304]{0:T(1024)(128)(4,1)S(1)}, s32[]{:S(2)}) async-start(s8[8388608]{0:T(1024)(128)(4,1)} %bitcast.6), calls=%async_computation.4 | async-start | bytes 8388608
  278.4 48.1 %slice-start.1 = ((s8[8388608]{0:T(1024)(128)(4,1)}), s8[4194304]{0:T(1024)(128)(4,1)S(1)}, s32[]{:S(2)}) async-start(s8[8388608]{0:T(1024)(128)(4,1)} %bitcast.6), calls=%async_computation.5 | async-start | bytes 8388608
Sparse Core Ops, SparseCore 0:
  24.4 54.5 all-gather.1
  105.9 170.0 reduce-scatter.1

commit v5 on v4

--- a/solution.py
+++ b/solution.py
@@ -18,43 +18,41 @@
     return (upstream * pre_up * curvature * tangent).astype(jnp.bfloat16)
 
 
-def products_kernel(n_ref, c_ref, wg_ref, wu_ref, pr_ref, wd_ref, o_ref):
-    f = wg_ref.shape[1]
-    n = n_ref[...]
-    for p, w_ref in enumerate((wg_ref, wu_ref, pr_ref)):
-        o_ref[0, :, p * f:(p + 1) * f] = jnp.dot(
-            n, w_ref[...], preferred_element_type=jnp.float32
-        ).astype(o_ref.dtype)
-    o_ref[0, :, 3 * f:4 * f] = lax.dot_general(
-        c_ref[...], wd_ref[...], (((1,), (1,)), ((), ())), preferred_element_type=jnp.float32
-    ).astype(o_ref.dtype)
+def products_kernel(n_ref, c_ref, *refs, pairs):
+    o_ref = refs[-1]
+    for p, (use_cot, w_ref) in enumerate(zip(pairs, refs[:-1])):
+        f = w_ref.shape[0] if use_cot else w_ref.shape[1]
+        if use_cot:
+            value = lax.dot_general(
+                c_ref[...], w_ref[...], (((1,), (1,)), ((), ())), preferred_element_type=jnp.float32
+            )
+        else:
+            value = jnp.dot(n_ref[...], w_ref[...], preferred_element_type=jnp.float32)
+        o_ref[0, :, p * f:(p + 1) * f] = value.astype(o_ref.dtype)
 
 
-def products(both, w_gate, w_up, probe, w_down, blocks):
+def products(both, weights, pairs, blocks):
     rows, width = both.shape[0], both.shape[1] // 2
-    f = w_gate.shape[1]
+    f = weights[0].shape[0] if pairs[0] else weights[0].shape[1]
     tm = rows // blocks
     full = lambda shape: pl.BlockSpec(shape, lambda i: (0, 0))
+    count = len(weights)
     return pl.pallas_call(
-        products_kernel,
-        out_shape=jax.ShapeDtypeStruct((blocks, tm, 4 * f), jnp.bfloat16),
+        functools.partial(products_kernel, pairs=tuple(pairs)),
+        out_shape=jax.ShapeDtypeStruct((blocks, tm, count * f), jnp.bfloat16),
         grid=(blocks,),
         in_specs=[
             pl.BlockSpec((tm, width), lambda i: (i, 0)),
             pl.BlockSpec((tm, width), lambda i: (i, 1)),
-            full(w_gate.shape),
-            full(w_up.shape),
-            full(probe.shape),
-            full(w_down.shape),
-        ],
-        out_specs=pl.BlockSpec((1, tm, 4 * f), lambda i: (i, 0, 0)),
+        ] + [full(w.shape) for w in weights],
+        out_specs=pl.BlockSpec((1, tm, count * f), lambda i: (i, 0, 0)),
         compiler_params=pltpu.CompilerParams(vmem_limit_bytes=48 * 1024 * 1024),
         cost_estimate=pl.CostEstimate(
-            flops=2 * rows * width * f * 4,
+            flops=2 * rows * width * f * count,
             transcendentals=0,
-            bytes_accessed=2 * (2 * rows * width + 4 * width * f + rows * 4 * f),
+            bytes_accessed=2 * (2 * rows * width + count * width * f + rows * count * f),
         ),
-    )(both, both, w_gate, w_up, probe, w_down)
+    )(both, both, *weights)
 
 
 def gather_tensor(x, axis):
@@ -83,13 +81,16 @@
     both = lax.all_gather(jnp.concatenate([normed_local, cotangent], axis=1), "seq", axis=0, tiled=True)
     total_tokens = both.shape[0]
     unit_count = w_gate.shape[1]
-    parts = products(both, w_gate, w_up, probe, w_down, n_tensor)
-    summed = lax.psum_scatter(parts, "tensor", scatter_dimension=0, tiled=True)[0].astype(jnp.float32)
+    first = products(both, (w_down, w_up), (True, False), n_tensor)
+    received = lax.all_to_all(first, "tensor", 0, 0, tiled=True)
+    rest = products(both, (w_gate, probe), (False, False), n_tensor)
+    scattered = lax.psum_scatter(rest, "tensor", scatter_dimension=0, tiled=True)[0].astype(jnp.float32)
+    summed = jnp.sum(received.astype(jnp.float32), axis=0)
     second = second_factor(
+        scattered[:, :unit_count],
+        summed[:, unit_count:],
+        scattered[:, unit_count:],
         summed[:, :unit_count],
-        summed[:, unit_count : 2 * unit_count],
-        summed[:, 2 * unit_count : 3 * unit_count],
-        summed[:, 3 * unit_count :],
     )
     product = lax.dot_general(
         both[:, :width],

time: 340 us -> 342 us (level)
  waiting for transfers between devices: 231 us -> 115 us
  blocking collectives: 47.6 us -> 158 us
  Pallas kernels: 22.2 us -> 26.8 us
    reduce_scatter x1, waiting for transfers between devices: 170 us -> 54.5 us  [body(): lax.psum_scatter(rest, 'tensor', scatter_dimension=0, tiled=True)[0]]
    all_to_all x0 -> x1, blocking collectives: none -> 111 us  [body(): received = lax.all_to_all(first, 'tensor', 0, 0, tiled=True)]
    pallas_call x1 -> x2, Pallas kernels: 22.2 us -> 26.8 us  [products(): pl.pallas_call(functools.partial(products_kernel, pairs=tuple(pairs)), ou...]
  transfers between devices with their start and end apart: 5 -> 5, of which waited for: 5 -> 5; matrix products, arithmetic and copies ran while one was open for 0% -> 0% of each run, Pallas kernels for 0% -> 4%
where the time goes in v5:
time: 342 us; the launch traced here: 341 us
  blocking collectives  158 us (46%)
  waiting for transfers between devices  115 us (34%)
  Pallas kernels  26.8 us (8%)
  between operations  13.5 us (4%)
  starting transfers between devices  8.25 us (2%)
  other arithmetic  6.8 us (2%)
  local copies, waits for them, and re-layouts  6.45 us (2%)
  matrix products  6.4 us (2%)
    all_to_all x1, blocking collectives, body(): received = lax.all_to_all(first, 'tensor', 0, 0, tiled=True)  111 us
    all_gather x1, waiting for transfers between devices, body(): lax.all_gather(jnp.concatenate([normed_local, cotangent], axis=1), 'seq',...  54.7 us
    reduce_scatter x1, waiting for transfers between devices, body(): lax.psum_scatter(rest, 'tensor', scatter_dimension=0, tiled=True)[0]  54.5 us
    all_to_all x1, blocking collectives, gather_tensor(): got = lax.all_to_all(repeated, axis, 0, 0, tiled=True)  47.5 us
    pallas_call x2, Pallas kernels, products(): pl.pallas_call(functools.partial(products_kernel, pairs=tuple(pairs)), ou...  26.8 us
    ppermute x3, starting transfers between devices, butterfly_sum(): x = x + lax.ppermute(x, axis, [(i, i ^ bit) for i in range(n)])  8.2 us
  transfers between devices with their start and end apart: 5, of which 5 were waited for; matrix products, arithmetic and copies ran while one was open for 0% of the time, Pallas kernels for 4%

profile of v5, /device:TPU:0, one launch (start us, length us, event | category | flops | bytes accessed | tf_op | source)
XLA Modules:
  0.0 340.9 jit_solution(2487925782763548952)
XLA Ops:
  6.5 0.0 all-gather.2.cloned.1.call-start
  6.5 1.1 fusion.9
  7.6 3.2 collective-permute-start
  10.8 1.9 collective-permute-done
  12.8 1.7 collective-permute-start.1
  14.5 1.9 collective-permute-done.1
  16.3 3.3 collective-permute-start.2
  19.6 1.8 collective-permute-done.2
  21.4 1.1 fusion.11
  22.5 1.8 pad_maximum_fusion
  24.3 0.0 all-gather.2.cloned.1.call-update
  24.3 0.0 reduce-scatter.2.cloned.1.call-start
  24.4 54.7 %all-gather.2.cloned.1.call-done.n_ref.c_ref = bf16[2048,2048]{1,0:T(8,128)(2,1)} async-done(((bf16[128,2048]{1,0:T(8,128)(2,1)}), bf16[2048,2048]{1,0:T(8,128)(2,1)}) %all-gather.2.cloned.1.call-update) | async-done | bytes 8388624 | tf_op jit(solution)/shard_map/all_gather | solution.py:81
  79.1 0.0 copy-start
  79.1 1.5 copy-done
  80.6 0.0 copy-start.1
  80.6 1.5 copy-done.1
  82.1 13.2 %shard_map.74 = bf16[8,256,1792]{2,1,0:T(8,128)(2,1)} custom-call(bf16[2048,2048]{1,0:T(8,128)(2,1)} %all-gather.2.cloned.1.call-done.n_ref.c_ref, bf16[2048,2048]{1,0:T(8,128)(2,1)} %all-gather.2.cloned.1.call-done.n_ref.c_ref, bf16[1024,896]{1,0:T(8,128)(2,1)S(1)} %copy-done, bf16[1024,896]{1,0:T(8,128)(2,1)S(1)} %copy-done.1), custom_call_target="tpu_custom_call" | custom-call | flops 7516192768 | bytes 19398656 | tf_op jit(solution)/shard_map/pallas_call | solution.py:40
  95.3 0.0 copy-start.2
  95.3 0.0 reduce-scatter.2.cloned.1.call-update
  95.3 1.5 copy-done.2
  96.8 0.0 copy-start.3
  96.8 1.5 copy-done.3
  98.3 13.5 %shard_map.73 = bf16[8,256,1792]{2,1,0:T(8,128)(2,1)} custom-call(bf16[2048,2048]{1,0:T(8,128)(2,1)} %all-gather.2.cloned.1.call-done.n_ref.c_ref, bf16[2048,2048]{1,0:T(8,128)(2,1)} %all-gather.2.cloned.1.call-done.n_ref.c_ref, bf16[896,1024]{1,0:T(8,128)(2,1)S(1)} %copy-done.2, bf16[1024,896]{1,0:T(8,128)(2,1)S(1)} %copy-done.3), custom_call_target="tpu_custom_call" | custom-call | flops 7516192768 | bytes 19398656 | tf_op jit(solution)/shard_map/pallas_call | solution.py:40
  111.8 110.5 %all_to_all.10 = bf16[8,256,1792]{2,1,0:T(8,128)(2,1)S(1)} all-to-all(bf16[8,256,1792]{2,1,0:T(8,128)(2,1)} %shard_map.73), channel_id=1, replica_groups=mesh['seq'=16,'tensor'=8] {'tensor'}, dimensions={0} | all-to-all | bytes 14680064 | tf_op jit(solution)/shard_map/all_to_all | solution.py:85
  222.3 1.0 convert_reduce_fusion
  223.4 54.5 %reduce-scatter.2.cloned.1.call-done = bf16[1,256,1792]{2,1,0:T(8,128)(2,1)} async-done(((bf16[8,256,1792]{2,1,0:T(8,128)(2,1)}), bf16[1,256,1792]{2,1,0:T(8,128)(2,1)}) %reduce-scatter.2.cloned.1.call-update) | async-done | bytes 917520 | tf_op jit(solution)/shard_map/reduce_scatter | solution.py:87
  277.9 1.3 bitcast_convert_fusion
  279.2 0.0 slice-start
  279.2 0.5 fusion.8
  279.7 0.0 slice-start.1
  279.7 0.5 broadcast_in_dim.2
  280.2 47.5 %all_to_all.11 = bf16[8,256,896]{2,1,0:T(8,128)(2,1)S(1)} all-to-all(bf16[8,256,896]{2,1,0:T(8,128)(2,1)S(1)} %broadcast_in_dim.2), channel_id=1, replica_groups=mesh['seq'=16,'tensor'=8] {'tensor'}, dimensions={0} | all-to-all | bytes 7340032 | tf_op jit(solution)/shard_map/all_to_all | solution.py:61
  327.7 0.0 slice-done
  327.7 0.0 slice-done.1
  327.7 6.4 %fusion.2 = f32[1024,896]{1,0:T(8,128)} fusion(bf16[2048,896]{1,0:T(8,128)(2,1)S(1)} %bitcast.5, bf16[2048,2048]{1,0:T(8,128)(2,1)S(1)} %bitcast.7), kind=kOutput, calls=%fused_computation.3 | convolution fusion | flops 3759013888 | bytes 11534336 | tf_op jit(solution)/shard_map/dot_general | solution.py:95
  (4 shorter events, 0.0 us)
Async XLA Ops:
  6.5 72.5 %all-gather.2.cloned.1.call-start = ((), (), s32[]{:S(2)}) async-start(), calls=%async_computation.3 | async-start | bytes 8912896 | tf_op jit(solution)/shard_map/all_gather | solution.py:81
  7.6 5.1 %collective-permute-start = (f32[128]{0:T(128)S(1)}, f32[128]{0:T(128)S(1)}, u32[]{:S(2)}, u32[]{:S(2)}) collective-permute-start(f32[128]{0:T(128)S(1)} %fusion.9), channel_id=1, source_target_pairs={{0,1},{1,0},{2,3},{3,2},{4,5},{5,4},{6,7},{7,6},{8,9},{9,8},{10,11... | collective-permute-start | bytes 1544 | tf_op jit(solution)/shard_map/ppermute | solution.py:69
  12.8 3.6 %collective-permute-start.1 = (f32[128]{0:T(128)S(1)}, f32[128]{0:T(128)S(1)}, u32[]{:S(2)}, u32[]{:S(2)}) collective-permute-start(f32[128]{0:T(128)S(1)} %add.23), channel_id=1, source_target_pairs={{0,2},{1,3},{2,0},{3,1},{4,6},{5,7},{6,4},{7,5},{8,10},{9,11},{10,... | collective-permute-start | bytes 1544 | tf_op jit(solution)/shard_map/ppermute | solution.py:69
  16.3 5.1 %collective-permute-start.2 = (f32[128]{0:T(128)S(1)}, f32[128]{0:T(128)S(1)}, u32[]{:S(2)}, u32[]{:S(2)}) collective-permute-start(f32[128]{0:T(128)S(1)} %add.24), channel_id=1, source_target_pairs={{0,4},{1,5},{2,6},{3,7},{4,0},{5,1},{6,2},{7,3},{8,12},{9,13},{10,... | collective-permute-start | bytes 1544 | tf_op jit(solution)/shard_map/ppermute | solution.py:69
  24.3 253.6 %reduce-scatter.2.cloned.1.call-start = ((), (), s32[]{:S(2)}) async-start(), calls=%async_computation.4 | async-start | bytes 8257536 | tf_op jit(solution)/shard_map/reduce_scatter | solution.py:87
  79.1 1.5 copy-start
  80.6 1.5 copy-start.1
  95.3 1.5 copy-start.2
  96.8 1.5 copy-start.3
  279.2 48.5 %slice-start = ((s8[8388608]{0:T(1024)(128)(4,1)}), s8[4194304]{0:T(1024)(128)(4,1)S(1)}, s32[]{:S(2)}) async-start(s8[8388608]{0:T(1024)(128)(4,1)} %bitcast.6), calls=%async_computation.5 | async-start | bytes 8388608
  279.7 48.0 %slice-start.1 = ((s8[8388608]{0:T(1024)(128)(4,1)}), s8[4194304]{0:T(1024)(128)(4,1)S(1)}, s32[]{:S(2)}) async-start(s8[8388608]{0:T(1024)(128)(4,1)} %bitcast.6), calls=%async_computation.6 | async-start | bytes 8388608
Sparse Core Ops, SparseCore 0:
  24.4 54.5 all-gather.1
  95.4 182.4 reduce-scatter.1

commit v6 on v4

--- a/solution.py
+++ b/solution.py
@@ -18,9 +18,10 @@
     return (upstream * pre_up * curvature * tangent).astype(jnp.bfloat16)
 
 
-def products_kernel(n_ref, c_ref, wg_ref, wu_ref, pr_ref, wd_ref, o_ref):
+def products_kernel(t_ref, c_ref, inv_ref, gain_ref, wg_ref, wu_ref, pr_ref, wd_ref, o_ref, n_out_ref):
     f = wg_ref.shape[1]
-    n = n_ref[...]
+    n = (t_ref[...].astype(jnp.float32) * inv_ref[...] * gain_ref[...]).astype(jnp.bfloat16)
+    n_out_ref[...] = n
     for p, w_ref in enumerate((wg_ref, wu_ref, pr_ref)):
         o_ref[0, :, p * f:(p + 1) * f] = jnp.dot(
             n, w_ref[...], preferred_element_type=jnp.float32
@@ -30,31 +31,39 @@
     ).astype(o_ref.dtype)
 
 
-def products(both, w_gate, w_up, probe, w_down, blocks):
+def products(both, inverse, gain, w_gate, w_up, probe, w_down, blocks):
     rows, width = both.shape[0], both.shape[1] // 2
     f = w_gate.shape[1]
     tm = rows // blocks
     full = lambda shape: pl.BlockSpec(shape, lambda i: (0, 0))
     return pl.pallas_call(
         products_kernel,
-        out_shape=jax.ShapeDtypeStruct((blocks, tm, 4 * f), jnp.bfloat16),
+        out_shape=(
+            jax.ShapeDtypeStruct((blocks, tm, 4 * f), jnp.bfloat16),
+            jax.ShapeDtypeStruct((rows, width), jnp.bfloat16),
+        ),
         grid=(blocks,),
         in_specs=[
             pl.BlockSpec((tm, width), lambda i: (i, 0)),
             pl.BlockSpec((tm, width), lambda i: (i, 1)),
+            pl.BlockSpec((tm, 1), lambda i: (i, 0)),
+            full((1, width)),
             full(w_gate.shape),
             full(w_up.shape),
             full(probe.shape),
             full(w_down.shape),
         ],
-        out_specs=pl.BlockSpec((1, tm, 4 * f), lambda i: (i, 0, 0)),
+        out_specs=(
+            pl.BlockSpec((1, tm, 4 * f), lambda i: (i, 0, 0)),
+            pl.BlockSpec((tm, width), lambda i: (i, 0)),
+        ),
         compiler_params=pltpu.CompilerParams(vmem_limit_bytes=48 * 1024 * 1024),
         cost_estimate=pl.CostEstimate(
             flops=2 * rows * width * f * 4,
             transcendentals=0,
-            bytes_accessed=2 * (2 * rows * width + 4 * width * f + rows * 4 * f),
+            bytes_accessed=2 * (3 * rows * width + 4 * width * f + rows * 4 * f),
         ),
-    )(both, both, w_gate, w_up, probe, w_down)
+    )(both, both, inverse.reshape(rows, 1), gain.reshape(1, width), w_gate, w_up, probe, w_down)
 
 
 def gather_tensor(x, axis):
@@ -76,14 +85,13 @@
 def body(tokens, cotangent, gain, w_gate, w_up, w_down, probe):
     n_tensor = lax.axis_size("tensor")
     width = tokens.shape[1]
+    both = lax.all_gather(jnp.concatenate([tokens, cotangent], axis=1), "seq", axis=0, tiled=True)
     values = tokens.astype(jnp.float32)
     squares = butterfly_sum(jnp.sum(values * values, axis=1), "tensor")
-    inverse = lax.rsqrt(squares / D + epsilon)
-    normed_local = (values * inverse[:, None] * gain[None, :]).astype(jnp.bfloat16)
-    both = lax.all_gather(jnp.concatenate([normed_local, cotangent], axis=1), "seq", axis=0, tiled=True)
+    inverse = gather_tensor(lax.rsqrt(squares / D + epsilon), "seq")
     total_tokens = both.shape[0]
     unit_count = w_gate.shape[1]
-    parts = products(both, w_gate, w_up, probe, w_down, n_tensor)
+    parts, normed = products(both, inverse, gain, w_gate, w_up, probe, w_down, n_tensor)
     summed = lax.psum_scatter(parts, "tensor", scatter_dimension=0, tiled=True)[0].astype(jnp.float32)
     second = second_factor(
         summed[:, :unit_count],
@@ -92,7 +100,7 @@
         summed[:, 3 * unit_count :],
     )
     product = lax.dot_general(
-        both[:, :width],
+        normed,
         gather_tensor(second, "tensor"),
         (((0,), (0,)), ((), ())),
         preferred_element_type=jnp.float32,

time: 340 us -> 325 us (0.956)
  waiting for transfers between devices: 231 us -> 203 us
  blocking collectives: 47.6 us -> 59.9 us
    all_gather x1, waiting for transfers between devices: 54.7 us -> 27.7 us  [body(): lax.all_gather(jnp.concatenate([tokens, cotangent], axis=1), 'seq', axis=...]
    all_to_all x1 -> x2, blocking collectives: 47.6 us -> 59.9 us  [gather_tensor(): got = lax.all_to_all(repeated, axis, 0, 0, tiled=True)]
where the time goes in v6:
time: 325 us
  waiting for transfers between devices  203 us (62%)
  blocking collectives  59.9 us (18%)
  Pallas kernels  23.4 us (7%)
  between operations  13.5 us (4%)
  starting transfers between devices  8.24 us (3%)
  matrix products  6.54 us (2%)
  other arithmetic  5.36 us (2%)
  local copies, waits for them, and re-layouts  4.53 us (1%)
    reduce_scatter x1, waiting for transfers between devices, body(): lax.psum_scatter(parts, 'tensor', scatter_dimension=0, tiled=True)[0]  170 us
    all_to_all x2, blocking collectives, gather_tensor(): got = lax.all_to_all(repeated, axis, 0, 0, tiled=True)  59.9 us
    all_gather x1, waiting for transfers between devices, body(): lax.all_gather(jnp.concatenate([tokens, cotangent], axis=1), 'seq', axis=...  27.7 us
    pallas_call x1, Pallas kernels, products(): pl.pallas_call(products_kernel, out_shape=(jax.ShapeDtypeStruct((blocks,...  23.4 us
    ppermute x3, starting transfers between devices, butterfly_sum(): x = x + lax.ppermute(x, axis, [(i, i ^ bit) for i in range(n)])  8.2 us
    dot_general x1, matrix products, body(): lax.dot_general(normed, gather_tensor(second, 'tensor'), (((0,), (0,)), (...  6.54 us
  transfers between devices with their start and end apart: 5, of which 5 were waited for; matrix products, arithmetic and copies ran while one was open for 0% of the time, Pallas kernels for 0%

profile of v6, /device:TPU:0, one launch (start us, length us, event | category | flops | bytes accessed | tf_op | source)
XLA Modules:
  0.0 325.0 jit_solution(8552899293341765892)
XLA Ops:
  6.5 0.0 all-gather.2.cloned.1.call-start
  6.5 1.9 pad_maximum_fusion
  8.4 0.0 all-gather.2.cloned.1.call-update
  8.4 0.0 reduce-scatter.2.cloned.1.call-start
  8.5 1.1 multiply_reduce_fusion
  9.6 3.2 collective-permute-start
  12.8 1.9 collective-permute-done
  14.7 1.7 collective-permute-start.1
  16.4 1.9 collective-permute-done.1
  18.3 3.3 %collective-permute-start.2 = (f32[128]{0:T(128)S(1)}, f32[128]{0:T(128)S(1)}, u32[]{:S(2)}, u32[]{:S(2)}) collective-permute-start(f32[128]{0:T(128)S(1)} %add.24), channel_id=1, source_target_pairs={{0,4},{1,5},{2,6},{3,7},{4,0},{5,1},{6,2},{7,3},{8,12},{9,13},{10,... | collective-permute-start | bytes 1544 | tf_op jit(solution)/shard_map/ppermute | solution.py:80
  21.6 1.8 collective-permute-done.2
  23.4 12.3 %all_to_all.11 = f32[16,1,128]{2,1,0:T(1,128)S(1)} all-to-all(f32[16,1,128]{2,1,0:T(1,128)S(1)} %broadcast_in_dim.4), channel_id=1, replica_groups=mesh['seq'=16,'tensor'=8] {'seq'}, dimensions={0} | all-to-all | bytes 16384 | tf_op jit(solution)/shard_map/all_to_all | solution.py:72
  35.7 0.4 copy.9.inv_ref
  36.1 27.7 %all-gather.2.cloned.1.call-done.t_ref.c_ref = bf16[2048,2048]{1,0:T(8,128)(2,1)} async-done(((bf16[128,2048]{1,0:T(8,128)(2,1)}), bf16[2048,2048]{1,0:T(8,128)(2,1)}) %all-gather.2.cloned.1.call-update) | async-done | bytes 8388624 | tf_op jit(solution)/shard_map/all_gather | solution.py:88
  63.7 0.0 copy-start
  63.7 1.5 copy-done
  65.2 0.0 copy-start.1
  65.2 1.5 copy-done.1
  66.7 0.0 copy-start.2
  66.7 0.7 copy-done.2
  67.4 23.4 %shard_map.73 = (bf16[8,256,3584]{2,1,0:T(8,128)(2,1)}, bf16[2048,1024]{1,0:T(8,128)(2,1)}) custom-call(bf16[2048,2048]{1,0:T(8,128)(2,1)} %all-gather.2.cloned.1.call-done.t_ref.c_ref, bf16[2048,2048]{1,0:T(8,128)(2,1)} %all-gather.2.cloned.1.call-done.t_ref.c_ref, f32[2048,1]{1,0:T(8,128)S(1)} %copy.9.inv_ref, f32[1,1024]{1,0:T(1,128)S(1)} %bitcast.8, ...), custom_call_target="tpu_custom_call" | custom-call | flops 15032385536 | bytes 34603008 | tf_op jit(solution)/shard_map/pallas_call | solution.py:39
  90.9 0.0 reduce-scatter.2.cloned.1.call-update
  90.9 170.2 %reduce-scatter.2.cloned.1.call-done = bf16[1,256,3584]{2,1,0:T(8,128)(2,1)} async-done(((bf16[8,256,3584]{2,1,0:T(8,128)(2,1)}), bf16[1,256,3584]{2,1,0:T(8,128)(2,1)}) %reduce-scatter.2.cloned.1.call-update) | async-done | bytes 1835024 | tf_op jit(solution)/shard_map/reduce_scatter | solution.py:95
  261.1 1.9 bitcast_convert_fusion
  263.0 0.5 fusion.3
  263.5 0.5 broadcast_in_dim.5
  264.0 0.0 copy-start.3
  264.0 47.6 %all_to_all.12 = bf16[8,256,896]{2,1,0:T(8,128)(2,1)S(1)} all-to-all(bf16[8,256,896]{2,1,0:T(8,128)(2,1)S(1)} %broadcast_in_dim.5), channel_id=1, replica_groups=mesh['seq'=16,'tensor'=8] {'tensor'}, dimensions={0} | all-to-all | bytes 7340032 | tf_op jit(solution)/shard_map/all_to_all | solution.py:72
  311.6 0.0 copy-done.3
  311.6 6.5 %convolution_multiply_fusion = f32[1024,896]{1,0:T(8,128)} fusion(bf16[2048,1024]{1,0:T(8,128)(2,1)S(1)} %copy-done.3, bf16[2048,896]{1,0:T(8,128)(2,1)S(1)} %bitcast.9), kind=kOutput, calls=%fused_computation | convolution fusion | flops 3759013888 | bytes 11534336 | tf_op jit(solution)/shard_map/dot_general | solution.py:102
  (4 shorter events, 0.0 us)
Async XLA Ops:
  6.5 57.2 %all-gather.2.cloned.1.call-start = ((), (), s32[]{:S(2)}) async-start(), calls=%async_computation.3 | async-start | bytes 8912896 | tf_op jit(solution)/shard_map/all_gather | solution.py:88
  8.4 252.7 %reduce-scatter.2.cloned.1.call-start = ((), (), s32[]{:S(2)}) async-start(), calls=%async_computation.4 | async-start | bytes 16515072 | tf_op jit(solution)/shard_map/reduce_scatter | solution.py:95
  9.6 5.1 %collective-permute-start = (f32[128]{0:T(128)S(1)}, f32[128]{0:T(128)S(1)}, u32[]{:S(2)}, u32[]{:S(2)}) collective-permute-start(f32[128]{0:T(128)S(1)} %multiply_reduce_fusion), channel_id=1, source_target_pairs={{0,1},{1,0},{2,3},{3,2},{4,5},{5,4},{6,7},{7,6},{8,9},{9,8},{10,11... | collective-permute-start | bytes 1544 | tf_op jit(solution)/shard_map/ppermute | solution.py:80
  14.7 3.6 %collective-permute-start.1 = (f32[128]{0:T(128)S(1)}, f32[128]{0:T(128)S(1)}, u32[]{:S(2)}, u32[]{:S(2)}) collective-permute-start(f32[128]{0:T(128)S(1)} %add.23), channel_id=1, source_target_pairs={{0,2},{1,3},{2,0},{3,1},{4,6},{5,7},{6,4},{7,5},{8,10},{9,11},{10,... | collective-permute-start | bytes 1544 | tf_op jit(solution)/shard_map/ppermute | solution.py:80
  18.3 5.1 %collective-permute-start.2 = (f32[128]{0:T(128)S(1)}, f32[128]{0:T(128)S(1)}, u32[]{:S(2)}, u32[]{:S(2)}) collective-permute-start(f32[128]{0:T(128)S(1)} %add.24), channel_id=1, source_target_pairs={{0,4},{1,5},{2,6},{3,7},{4,0},{5,1},{6,2},{7,3},{8,12},{9,13},{10,... | collective-permute-start | bytes 1544 | tf_op jit(solution)/shard_map/ppermute | solution.py:80
  63.7 1.5 copy-start
  65.2 1.5 copy-start.1
  66.7 0.7 copy-start.2
  264.0 47.6 %copy-start.3 = (bf16[2048,1024]{1,0:T(8,128)(2,1)S(1)}, bf16[2048,1024]{1,0:T(8,128)(2,1)}, u32[]{:S(2)}) copy-start(bf16[2048,1024]{1,0:T(8,128)(2,1)} %get-tuple-element.7) | copy-start | bytes 12582916
Sparse Core Ops, SparseCore 0:
  9.0 54.6 all-gather.1
  91.0 170.0 reduce-scatter.1

commit v7 on v6

--- a/solution.py
+++ b/solution.py
@@ -1,11 +1,10 @@
-import functools
-
 import jax
 import jax.numpy as jnp
 from jax import lax
 from jax.experimental import pallas as pl
 from jax.experimental.pallas import tpu as pltpu
-from jax.sharding import PartitionSpec as P
+from jax.sharding import Mesh, PartitionSpec as P
+
 
 D = 8192
 
@@ -82,17 +81,28 @@
     return x
 
 
+SEQ = ("xl", "z", "c")
+TEN = ("y", "xh")
+
+
 def body(tokens, cotangent, gain, w_gate, w_up, w_down, probe):
-    n_tensor = lax.axis_size("tensor")
-    width = tokens.shape[1]
-    both = lax.all_gather(jnp.concatenate([tokens, cotangent], axis=1), "seq", axis=0, tiled=True)
+    n_tensor = lax.axis_size(TEN)
+    local_rows = tokens.shape[0]
+    core = lax.axis_index("c")
+    own = lax.all_gather(jnp.concatenate([tokens, cotangent], axis=1), ("xl", "z"), axis=0, tiled=True)
+    other = lax.ppermute(own, "c", [(0, 1), (1, 0)])
+    both = jnp.concatenate([own, other], axis=0)
     values = tokens.astype(jnp.float32)
-    squares = butterfly_sum(jnp.sum(values * values, axis=1), "tensor")
-    inverse = gather_tensor(lax.rsqrt(squares / D + epsilon), "seq")
+    squares = butterfly_sum(jnp.sum(values * values, axis=1), TEN)
+    inverse = gather_tensor(lax.rsqrt(squares / D + epsilon), SEQ).reshape(-1, 2, local_rows)
+    inverse = jnp.concatenate(
+        [lax.dynamic_index_in_dim(inverse, core, 1, keepdims=False),
+         lax.dynamic_index_in_dim(inverse, 1 - core, 1, keepdims=False)], axis=0
+    ).reshape(-1)
     total_tokens = both.shape[0]
     unit_count = w_gate.shape[1]
     parts, normed = products(both, inverse, gain, w_gate, w_up, probe, w_down, n_tensor)
-    summed = lax.psum_scatter(parts, "tensor", scatter_dimension=0, tiled=True)[0].astype(jnp.float32)
+    summed = lax.psum_scatter(parts, TEN, scatter_dimension=0, tiled=True)[0].astype(jnp.float32)
     second = second_factor(
         summed[:, :unit_count],
         summed[:, unit_count : 2 * unit_count],
@@ -101,7 +111,7 @@
     )
     product = lax.dot_general(
         normed,
-        gather_tensor(second, "tensor"),
+        gather_tensor(second, TEN),
         (((0,), (0,)), ((), ())),
         preferred_element_type=jnp.float32,
     )
@@ -109,18 +119,22 @@
 
 
 def solution(mesh):
+    seq_size, tensor_size = mesh.devices.shape
+    mesh5 = Mesh(
+        mesh.devices.reshape(seq_size // 8, 4, 2, tensor_size // 2, 2), SEQ + TEN
+    )
     return jax.shard_map(
         body,
-        mesh=mesh,
+        mesh=mesh5,
         in_specs=(
-            P("seq", "tensor"),
-            P("seq", "tensor"),
-            P("tensor"),
-            P("tensor", "seq"),
-            P("tensor", "seq"),
-            P("seq", "tensor"),
-            P("tensor", "seq"),
+            P(SEQ, TEN),
+            P(SEQ, TEN),
+            P(TEN),
+            P(TEN, SEQ),
+            P(TEN, SEQ),
+            P(SEQ, TEN),
+            P(TEN, SEQ),
         ),
-        out_specs=P("tensor", "seq"),
+        out_specs=P(TEN, SEQ),
         check_vma=False,
     )

time: 325 us -> 355 us (1.092)
  waiting for transfers between devices: 203 us -> 237 us
  blocking collectives: 59.9 us -> 47.6 us
  other arithmetic: 5.36 us -> 13.9 us
    all_gather x1, waiting for transfers between devices: 27.7 us -> 55.8 us  [body(): lax.all_gather(jnp.concatenate([tokens, cotangent], axis=1), ('xl', 'z'),...]
    all_to_all x2 -> x1, blocking collectives: 59.9 us -> 47.6 us  [gather_tensor(): got = lax.all_to_all(repeated, axis, 0, 0, tiled=True)]
    concatenate x0 -> x2, other arithmetic: none -> 8.52 us  [the longest x1 8.52 us: body(): both = jnp.concatenate([own, other], axis=0)]
    all_to_all x0 -> x1, waiting for transfers between devices: none -> 5.9 us  [gather_tensor(): got = lax.all_to_all(repeated, axis, 0, 0, tiled=True)]
  transfers between devices with their start and end apart: 5 -> 7, of which waited for: 5 -> 6; matrix products, arithmetic and copies ran while one was open for 0% -> 1% of each run, Pallas kernels for 0% -> 0%
where the time goes in v7:
time: 355 us
  waiting for transfers between devices  237 us (67%)
  blocking collectives  47.6 us (13%)
  Pallas kernels  23.4 us (7%)
  other arithmetic  13.9 us (4%)
  between operations  13.5 us (4%)
  starting transfers between devices  10.8 us (3%)
  matrix products  6.54 us (2%)
    reduce_scatter x1, waiting for transfers between devices, body(): lax.psum_scatter(parts, TEN, scatter_dimension=0, tiled=True)[0]  168 us
    all_gather x1, waiting for transfers between devices, body(): lax.all_gather(jnp.concatenate([tokens, cotangent], axis=1), ('xl', 'z'),...  55.8 us
    all_to_all x1, blocking collectives, gather_tensor(): got = lax.all_to_all(repeated, axis, 0, 0, tiled=True)  47.6 us
    pallas_call x1, Pallas kernels, products(): pl.pallas_call(products_kernel, out_shape=(jax.ShapeDtypeStruct((blocks,...  23.4 us
    concatenate x1, other arithmetic, body(): both = jnp.concatenate([own, other], axis=0)  8.52 us
    ppermute x3, starting transfers between devices, butterfly_sum(): x = x + lax.ppermute(x, axis, [(i, i ^ bit) for i in range(n)])  7.26 us
  transfers between devices with their start and end apart: 7, of which 6 were waited for; matrix products, arithmetic and copies ran while one was open for 1% of the time, Pallas kernels for 0%

profile of v7, /device:TPU:0, one launch (start us, length us, event | category | flops | bytes accessed | tf_op | source)
XLA Modules:
  0.0 355.2 jit_solution(5718465962046303129)
XLA Ops:
  6.5 0.0 all-gather.2.cloned.1.call-start
  6.5 1.9 pad_maximum_fusion.1
  8.4 0.0 all-gather.2.cloned.1.call-update
  8.4 55.8 %all-gather.2.cloned.1.call-done = bf16[1024,2048]{1,0:T(8,128)(2,1)} async-done(((bf16[128,2048]{1,0:T(8,128)(2,1)}), bf16[1024,2048]{1,0:T(8,128)(2,1)}) %all-gather.2.cloned.1.call-update) | async-done | bytes 4194320 | tf_op jit(solution)/shard_map/all_gather | solution.py:92
  64.2 0.0 collective-permute-start
  64.2 1.1 multiply_reduce_fusion
  65.3 2.8 collective-permute-start.1
  68.1 2.4 collective-permute-done.1
  70.5 1.5 collective-permute-start.2
  72.0 2.1 collective-permute-done.2
  74.0 3.0 collective-permute-start.3
  77.1 2.1 collective-permute-done.3
  79.1 0.6 broadcast_in_dim.4
  79.7 3.5 all-to-all-start
  83.2 0.0 reduce-scatter.2.cloned.1.call-start
  83.3 5.9 %all-to-all-done = f32[16,1,128]{2,1,0:T(1,128)S(1)} async-done(((f32[16,1,128]{2,1,0:T(1,128)}), f32[16,1,128]{2,1,0:T(1,128)S(1)}, u32[]{:S(2)}, u32[]{:S(2)}) %all-to-all-start) | async-done | bytes 8224 | tf_op jit(solution)/shard_map/all_to_all | solution.py:71
  89.2 0.4 copy.9.inv_ref
  89.6 0.0 copy-start
  89.6 0.0 copy-start.2
  89.6 0.0 collective-permute-done
  89.6 8.5 %pad_maximum_fusion.t_ref.c_ref = bf16[2048,2048]{1,0:T(8,128)(2,1)} fusion(bf16[1024,2048]{1,0:T(8,128)(2,1)} %collective-permute-done, bf16[1024,2048]{1,0:T(8,128)(2,1)} %all-gather.2.cloned.1.call-done), kind=kLoop, calls=%fused_computation | loop fusion | flops 16777216 | bytes 16777216 | tf_op jit(solution)/shard_map/concatenate | solution.py:94
  98.1 0.0 copy-done
  98.1 0.0 copy-done.2
  98.1 0.0 copy-start.1
  98.1 1.5 copy-done.1
  99.6 23.4 %shard_map.73 = (bf16[8,256,3584]{2,1,0:T(8,128)(2,1)}, bf16[2048,1024]{1,0:T(8,128)(2,1)}) custom-call(bf16[2048,2048]{1,0:T(8,128)(2,1)} %pad_maximum_fusion.t_ref.c_ref, bf16[2048,2048]{1,0:T(8,128)(2,1)} %pad_maximum_fusion.t_ref.c_ref, f32[2048,1]{1,0:T(8,128)S(1)} %copy.9.inv_ref, f32[1,1024]{1,0:T(1,128)S(1)} %bitcast.11, ...), custom_call_target="tpu_custom_call" | custom-call | flops 15032385536 | bytes 34603008 | tf_op jit(solution)/shard_map/pallas_call | solution.py:38
  123.1 0.0 reduce-scatter.2.cloned.1.call-update
  123.1 168.3 %reduce-scatter.2.cloned.1.call-done = bf16[1,256,3584]{2,1,0:T(8,128)(2,1)} async-done(((bf16[8,256,3584]{2,1,0:T(8,128)(2,1)}), bf16[1,256,3584]{2,1,0:T(8,128)(2,1)}) %reduce-scatter.2.cloned.1.call-update) | async-done | bytes 1835024 | tf_op jit(solution)/shard_map/reduce_scatter | solution.py:105
  291.3 1.9 bitcast_convert_fusion
  293.3 0.5 fusion.3
  293.8 0.5 broadcast_in_dim.5
  294.2 0.0 copy-start.3
  294.3 47.6 %all_to_all.11 = bf16[8,256,896]{2,1,0:T(8,128)(2,1)S(1)} all-to-all(bf16[8,256,896]{2,1,0:T(8,128)(2,1)S(1)} %broadcast_in_dim.5), channel_id=1, replica_groups=mesh['xl'=2,'z'=4,'c'=2,'y'=4,'xh'=2] {'y','xh'}, dimensions={0} | all-to-all | bytes 7340032 | tf_op jit(solution)/shard_map/all_to_all | solution.py:71
  341.8 0.0 copy-done.3
  341.8 6.5 %convolution_multiply_fusion = f32[1024,896]{1,0:T(8,128)} fusion(bf16[2048,1024]{1,0:T(8,128)(2,1)S(1)} %copy-done.3, bf16[2048,896]{1,0:T(8,128)(2,1)S(1)} %bitcast.12), kind=kOutput, calls=%fused_computation.1 | convolution fusion | flops 3759013888 | bytes 11534336 | tf_op jit(solution)/shard_map/dot_general | solution.py:112
  (5 shorter events, 0.0 us)
Async XLA Ops:
  6.5 57.7 %all-gather.2.cloned.1.call-start = ((), (), s32[]{:S(2)}) async-start(), calls=%async_computation.3 | async-start | bytes 4718592 | tf_op jit(solution)/shard_map/all_gather | solution.py:92
  64.2 25.4 %collective-permute-start = (bf16[1024,2048]{1,0:T(8,128)(2,1)}, bf16[1024,2048]{1,0:T(8,128)(2,1)}, u32[]{:S(2)}, u32[]{:S(2)}) collective-permute-start(bf16[1024,2048]{1,0:T(8,128)(2,1)} %all-gather.2.cloned.1.call-done), channel_id=1, source_target_pairs={{0,8},{8,0},{1,9},{9,1},{2,10},{10,2},{3,11},{11,3},{4,12},{12,4},... | collective-permute-start | bytes 12582920 | tf_op jit(solution)/shard_map/ppermute | solution.py:93
  65.3 5.1 %collective-permute-start.1 = (f32[128]{0:T(128)S(1)}, f32[128]{0:T(128)S(1)}, u32[]{:S(2)}, u32[]{:S(2)}) collective-permute-start(f32[128]{0:T(128)S(1)} %multiply_reduce_fusion), channel_id=1, source_target_pairs={{0,1},{1,0},{2,3},{3,2},{4,5},{5,4},{6,7},{7,6},{8,9},{9,8},{10,11... | collective-permute-start | bytes 1544 | tf_op jit(solution)/shard_map/ppermute | solution.py:79
  70.5 3.6 %collective-permute-start.2 = (f32[128]{0:T(128)S(1)}, f32[128]{0:T(128)S(1)}, u32[]{:S(2)}, u32[]{:S(2)}) collective-permute-start(f32[128]{0:T(128)S(1)} %add.31), channel_id=1, source_target_pairs={{0,2},{1,3},{2,0},{3,1},{4,6},{5,7},{6,4},{7,5},{8,10},{9,11},{10,... | collective-permute-start | bytes 1544 | tf_op jit(solution)/shard_map/ppermute | solution.py:79
  74.0 5.1 %collective-permute-start.3 = (f32[128]{0:T(128)S(1)}, f32[128]{0:T(128)S(1)}, u32[]{:S(2)}, u32[]{:S(2)}) collective-permute-start(f32[128]{0:T(128)S(1)} %add.32), channel_id=1, source_target_pairs={{0,4},{1,5},{2,6},{3,7},{4,0},{5,1},{6,2},{7,3},{8,12},{9,13},{10,... | collective-permute-start | bytes 1544 | tf_op jit(solution)/shard_map/ppermute | solution.py:79
  79.7 9.4 %all-to-all-start = ((f32[16,1,128]{2,1,0:T(1,128)}), f32[16,1,128]{2,1,0:T(1,128)S(1)}, u32[]{:S(2)}, u32[]{:S(2)}) async-start(f32[16,1,128]{2,1,0:T(1,128)} %broadcast_in_dim.4), calls=%async_computation | async-start | bytes 16384 | tf_op jit(solution)/shard_map/all_to_all | solution.py:71
  83.2 208.1 %reduce-scatter.2.cloned.1.call-start = ((), (), s32[]{:S(2)}) async-start(), calls=%async_computation.4 | async-start | bytes 16515072 | tf_op jit(solution)/shard_map/reduce_scatter | solution.py:105
  89.6 8.6 %copy-start = (bf16[1024,896]{1,0:T(8,128)(2,1)S(1)}, bf16[1024,896]{1,0:T(8,128)(2,1)}, u32[]{:S(2)}) copy-start(bf16[1024,896]{1,0:T(8,128)(2,1)} %wg_ref.1) | copy-start | bytes 5505028
  89.6 8.5 %copy-start.2 = (f32[1024]{0:T(1024)S(1)}, f32[1024]{0:T(1024)}, u32[]{:S(2)}) copy-start(f32[1024]{0:T(1024)} %param.9) | copy-start | bytes 12292
  98.1 1.5 copy-start.1
  294.2 47.6 %copy-start.3 = (bf16[2048,1024]{1,0:T(8,128)(2,1)S(1)}, bf16[2048,1024]{1,0:T(8,128)(2,1)}, u32[]{:S(2)}) copy-start(bf16[2048,1024]{1,0:T(8,128)(2,1)} %get-tuple-element.7) | copy-start | bytes 12582916
Sparse Core Ops, SparseCore 0:
  9.0 55.2 all-gather.1
  123.2 168.0 reduce-scatter.1

commit v8 on v6

--- a/solution.py
+++ b/solution.py
@@ -18,14 +18,37 @@
     return (upstream * pre_up * curvature * tangent).astype(jnp.bfloat16)
 
 
-def products_kernel(t_ref, c_ref, inv_ref, gain_ref, wg_ref, wu_ref, pr_ref, wd_ref, o_ref, n_out_ref):
+def products_kernel(t_ref, c_ref, inv_ref, gain_ref, wg_hbm, wu_hbm, pr_hbm, wd_hbm, o_ref, n_out_ref,
+                    wg_ref, wu_ref, pr_ref, wd_ref, sems):
+    first = pl.program_id(0) == 0
+    copies = [
+        pltpu.make_async_copy(src, dst, sems.at[k])
+        for k, (src, dst) in enumerate(
+            ((wg_hbm, wg_ref), (wu_hbm, wu_ref), (pr_hbm, pr_ref), (wd_hbm, wd_ref))
+        )
+    ]
+
+    @pl.when(first)
+    def _():
+        for copy in copies:
+            copy.start()
+
     f = wg_ref.shape[1]
     n = (t_ref[...].astype(jnp.float32) * inv_ref[...] * gain_ref[...]).astype(jnp.bfloat16)
     n_out_ref[...] = n
     for p, w_ref in enumerate((wg_ref, wu_ref, pr_ref)):
+        @pl.when(first)
+        def _():
+            copies[p].wait()
+
         o_ref[0, :, p * f:(p + 1) * f] = jnp.dot(
             n, w_ref[...], preferred_element_type=jnp.float32
         ).astype(o_ref.dtype)
+
+    @pl.when(first)
+    def _():
+        copies[3].wait()
+
     o_ref[0, :, 3 * f:4 * f] = lax.dot_general(
         c_ref[...], wd_ref[...], (((1,), (1,)), ((), ())), preferred_element_type=jnp.float32
     ).astype(o_ref.dtype)
@@ -35,7 +58,7 @@
     rows, width = both.shape[0], both.shape[1] // 2
     f = w_gate.shape[1]
     tm = rows // blocks
-    full = lambda shape: pl.BlockSpec(shape, lambda i: (0, 0))
+    hbm = pl.BlockSpec(memory_space=pltpu.HBM)
     return pl.pallas_call(
         products_kernel,
         out_shape=(
@@ -47,17 +70,24 @@
             pl.BlockSpec((tm, width), lambda i: (i, 0)),
             pl.BlockSpec((tm, width), lambda i: (i, 1)),
             pl.BlockSpec((tm, 1), lambda i: (i, 0)),
-            full((1, width)),
-            full(w_gate.shape),
-            full(w_up.shape),
-            full(probe.shape),
-            full(w_down.shape),
+            pl.BlockSpec((1, width), lambda i: (0, 0)),
+            hbm,
+            hbm,
+            hbm,
+            hbm,
         ],
         out_specs=(
             pl.BlockSpec((1, tm, 4 * f), lambda i: (i, 0, 0)),
             pl.BlockSpec((tm, width), lambda i: (i, 0)),
         ),
-        compiler_params=pltpu.CompilerParams(vmem_limit_bytes=48 * 1024 * 1024),
+        scratch_shapes=[
+            pltpu.VMEM(w_gate.shape, w_gate.dtype),
+            pltpu.VMEM(w_up.shape, w_up.dtype),
+            pltpu.VMEM(probe.shape, probe.dtype),
+            pltpu.VMEM(w_down.shape, w_down.dtype),
+            pltpu.SemaphoreType.DMA((4,)),
+        ],
+        compiler_params=pltpu.CompilerParams(dimension_semantics=("arbitrary",)),
         cost_estimate=pl.CostEstimate(
             flops=2 * rows * width * f * 4,
             transcendentals=0,

time: 325 us -> 327 us (level)
  Pallas kernels: 23.4 us -> 28.9 us
    pallas_call x1, Pallas kernels: 23.4 us -> 28.9 us  [products(): pl.pallas_call(products_kernel, out_shape=(jax.ShapeDtypeStruct((blocks,...]
    unnamed x8 -> x2, local copies, waits for them, and re-layouts: 3.69 us -> 0.01 us
  transfers between devices with their start and end apart: 5 -> 5, of which waited for: 5 -> 5; matrix products, arithmetic and copies ran while one was open for 0% -> 1% of each run, Pallas kernels for 0% -> 0%
where the time goes in v8:
time: 327 us
  waiting for transfers between devices  203 us (62%)
  blocking collectives  59.9 us (18%)
  Pallas kernels  28.9 us (9%)
  between operations  13.4 us (4%)
  starting transfers between devices  8.24 us (3%)
  matrix products  6.54 us (2%)
  other arithmetic  5.36 us (2%)
    reduce_scatter x1, waiting for transfers between devices, body(): lax.psum_scatter(parts, 'tensor', scatter_dimension=0, tiled=True)[0]  170 us
    all_to_all x2, blocking collectives, gather_tensor(): got = lax.all_to_all(repeated, axis, 0, 0, tiled=True)  59.9 us
    pallas_call x1, Pallas kernels, products(): pl.pallas_call(products_kernel, out_shape=(jax.ShapeDtypeStruct((blocks,...  28.9 us
    all_gather x1, waiting for transfers between devices, body(): lax.all_gather(jnp.concatenate([tokens, cotangent], axis=1), 'seq', axis=...  26.7 us
    ppermute x3, starting transfers between devices, butterfly_sum(): x = x + lax.ppermute(x, axis, [(i, i ^ bit) for i in range(n)])  8.2 us
  transfers between devices with their start and end apart: 5, of which 5 were waited for; matrix products, arithmetic and copies ran while one was open for 1% of the time, Pallas kernels for 0%

profile of v8, /device:TPU:0, one launch (start us, length us, event | category | flops | bytes accessed | tf_op | source)
XLA Modules:
  0.0 326.8 jit_solution(8010403269697148890)
XLA Ops:
  6.5 0.0 all-gather.2.cloned.1.call-start
  6.5 1.9 pad_maximum_fusion
  8.4 0.0 all-gather.2.cloned.1.call-update
  8.4 0.0 reduce-scatter.2.cloned.1.call-start
  8.5 1.1 multiply_reduce_fusion
  9.6 3.2 collective-permute-start
  12.8 1.9 collective-permute-done
  14.7 1.7 collective-permute-start.1
  16.4 1.9 collective-permute-done.1
  18.3 3.3 %collective-permute-start.2 = (f32[128]{0:T(128)S(1)}, f32[128]{0:T(128)S(1)}, u32[]{:S(2)}, u32[]{:S(2)}) collective-permute-start(f32[128]{0:T(128)S(1)} %add.24), channel_id=1, source_target_pairs={{0,4},{1,5},{2,6},{3,7},{4,0},{5,1},{6,2},{7,3},{8,12},{9,13},{10,... | collective-permute-start | bytes 1544 | tf_op jit(solution)/shard_map/ppermute | solution.py:110
  21.6 1.8 collective-permute-done.2
  23.4 12.3 %all_to_all.11 = f32[16,1,128]{2,1,0:T(1,128)S(1)} all-to-all(f32[16,1,128]{2,1,0:T(1,128)S(1)} %broadcast_in_dim.4), channel_id=1, replica_groups=mesh['seq'=16,'tensor'=8] {'seq'}, dimensions={0} | all-to-all | bytes 16384 | tf_op jit(solution)/shard_map/all_to_all | solution.py:102
  35.7 1.3 copy.9.inv_ref
  37.0 26.7 %all-gather.2.cloned.1.call-done.t_ref.c_ref = bf16[2048,2048]{1,0:T(8,128)(2,1)} async-done(((bf16[128,2048]{1,0:T(8,128)(2,1)}), bf16[2048,2048]{1,0:T(8,128)(2,1)}) %all-gather.2.cloned.1.call-update) | async-done | bytes 8388624 | tf_op jit(solution)/shard_map/all_gather | solution.py:118
  63.7 28.9 %shard_map.73 = (bf16[8,256,3584]{2,1,0:T(8,128)(2,1)}, bf16[2048,1024]{1,0:T(8,128)(2,1)}) custom-call(bf16[2048,2048]{1,0:T(8,128)(2,1)} %all-gather.2.cloned.1.call-done.t_ref.c_ref, bf16[2048,2048]{1,0:T(8,128)(2,1)} %all-gather.2.cloned.1.call-done.t_ref.c_ref, f32[2048,1]{1,0:T(8,128)} %copy.9.inv_ref, f32[1,1024]{1,0:T(1,128)} %bitcast.10, ...), custom_call_target="tpu_custom_call" | custom-call | flops 15032385536 | bytes 34603008 | tf_op jit(solution)/shard_map/pallas_call | solution.py:62
  92.6 0.0 reduce-scatter.2.cloned.1.call-update
  92.7 170.2 %reduce-scatter.2.cloned.1.call-done = bf16[1,256,3584]{2,1,0:T(8,128)(2,1)} async-done(((bf16[8,256,3584]{2,1,0:T(8,128)(2,1)}), bf16[1,256,3584]{2,1,0:T(8,128)(2,1)}) %reduce-scatter.2.cloned.1.call-update) | async-done | bytes 1835024 | tf_op jit(solution)/shard_map/reduce_scatter | solution.py:125
  262.9 1.9 bitcast_convert_fusion
  264.8 0.5 fusion.3
  265.3 0.5 broadcast_in_dim.5
  265.8 0.0 copy-start
  265.8 47.6 %all_to_all.12 = bf16[8,256,896]{2,1,0:T(8,128)(2,1)S(1)} all-to-all(bf16[8,256,896]{2,1,0:T(8,128)(2,1)S(1)} %broadcast_in_dim.5), channel_id=1, replica_groups=mesh['seq'=16,'tensor'=8] {'tensor'}, dimensions={0} | all-to-all | bytes 7340032 | tf_op jit(solution)/shard_map/all_to_all | solution.py:102
  313.4 0.0 copy-done
  313.4 6.5 %convolution_multiply_fusion = f32[1024,896]{1,0:T(8,128)} fusion(bf16[2048,1024]{1,0:T(8,128)(2,1)S(1)} %copy-done, bf16[2048,896]{1,0:T(8,128)(2,1)S(1)} %bitcast.8), kind=kOutput, calls=%fused_computation | convolution fusion | flops 3759013888 | bytes 11534336 | tf_op jit(solution)/shard_map/dot_general | solution.py:132
  (4 shorter events, 0.0 us)
Async XLA Ops:
  6.5 57.2 %all-gather.2.cloned.1.call-start = ((), (), s32[]{:S(2)}) async-start(), calls=%async_computation.3 | async-start | bytes 8912896 | tf_op jit(solution)/shard_map/all_gather | solution.py:118
  8.4 254.5 %reduce-scatter.2.cloned.1.call-start = ((), (), s32[]{:S(2)}) async-start(), calls=%async_computation.4 | async-start | bytes 16515072 | tf_op jit(solution)/shard_map/reduce_scatter | solution.py:125
  9.6 5.1 %collective-permute-start = (f32[128]{0:T(128)S(1)}, f32[128]{0:T(128)S(1)}, u32[]{:S(2)}, u32[]{:S(2)}) collective-permute-start(f32[128]{0:T(128)S(1)} %multiply_reduce_fusion), channel_id=1, source_target_pairs={{0,1},{1,0},{2,3},{3,2},{4,5},{5,4},{6,7},{7,6},{8,9},{9,8},{10,11... | collective-permute-start | bytes 1544 | tf_op jit(solution)/shard_map/ppermute | solution.py:110
  14.7 3.6 %collective-permute-start.1 = (f32[128]{0:T(128)S(1)}, f32[128]{0:T(128)S(1)}, u32[]{:S(2)}, u32[]{:S(2)}) collective-permute-start(f32[128]{0:T(128)S(1)} %add.23), channel_id=1, source_target_pairs={{0,2},{1,3},{2,0},{3,1},{4,6},{5,7},{6,4},{7,5},{8,10},{9,11},{10,... | collective-permute-start | bytes 1544 | tf_op jit(solution)/shard_map/ppermute | solution.py:110
  18.3 5.1 %collective-permute-start.2 = (f32[128]{0:T(128)S(1)}, f32[128]{0:T(128)S(1)}, u32[]{:S(2)}, u32[]{:S(2)}) collective-permute-start(f32[128]{0:T(128)S(1)} %add.24), channel_id=1, source_target_pairs={{0,4},{1,5},{2,6},{3,7},{4,0},{5,1},{6,2},{7,3},{8,12},{9,13},{10,... | collective-permute-start | bytes 1544 | tf_op jit(solution)/shard_map/ppermute | solution.py:110
  265.8 47.6 %copy-start = (bf16[2048,1024]{1,0:T(8,128)(2,1)S(1)}, bf16[2048,1024]{1,0:T(8,128)(2,1)}, u32[]{:S(2)}) copy-start(bf16[2048,1024]{1,0:T(8,128)(2,1)} %get-tuple-element.7) | copy-start | bytes 12582916
Sparse Core Ops, SparseCore 0:
  9.0 54.6 all-gather.1
  92.8 170.0 reduce-scatter.1

commit v9 on v6

--- a/solution.py
+++ b/solution.py
@@ -20,29 +20,33 @@
 
 def products_kernel(t_ref, c_ref, inv_ref, gain_ref, wg_ref, wu_ref, pr_ref, wd_ref, o_ref, n_out_ref):
     f = wg_ref.shape[1]
+    split, part = o_ref.shape[0], o_ref.shape[1]
     n = (t_ref[...].astype(jnp.float32) * inv_ref[...] * gain_ref[...]).astype(jnp.bfloat16)
     n_out_ref[...] = n
-    for p, w_ref in enumerate((wg_ref, wu_ref, pr_ref)):
-        o_ref[0, :, p * f:(p + 1) * f] = jnp.dot(
-            n, w_ref[...], preferred_element_type=jnp.float32
-        ).astype(o_ref.dtype)
-    o_ref[0, :, 3 * f:4 * f] = lax.dot_general(
-        c_ref[...], wd_ref[...], (((1,), (1,)), ((), ())), preferred_element_type=jnp.float32
-    ).astype(o_ref.dtype)
+    values = [jnp.dot(n, w_ref[...], preferred_element_type=jnp.float32) for w_ref in (wg_ref, wu_ref, pr_ref)]
+    values.append(
+        lax.dot_general(
+            c_ref[...], wd_ref[...], (((1,), (1,)), ((), ())), preferred_element_type=jnp.float32
+        )
+    )
+    for p, value in enumerate(values):
+        for j in range(split):
+            o_ref[j, :, p * f:(p + 1) * f] = value[j * part:(j + 1) * part].astype(o_ref.dtype)
 
 
-def products(both, inverse, gain, w_gate, w_up, probe, w_down, blocks):
+def products(both, inverse, gain, w_gate, w_up, probe, w_down, blocks, split=2):
     rows, width = both.shape[0], both.shape[1] // 2
     f = w_gate.shape[1]
-    tm = rows // blocks
+    part = rows // blocks
+    tm = part * split
     full = lambda shape: pl.BlockSpec(shape, lambda i: (0, 0))
     return pl.pallas_call(
         products_kernel,
         out_shape=(
-            jax.ShapeDtypeStruct((blocks, tm, 4 * f), jnp.bfloat16),
+            jax.ShapeDtypeStruct((blocks, part, 4 * f), jnp.bfloat16),
             jax.ShapeDtypeStruct((rows, width), jnp.bfloat16),
         ),
-        grid=(blocks,),
+        grid=(blocks // split,),
         in_specs=[
             pl.BlockSpec((tm, width), lambda i: (i, 0)),
             pl.BlockSpec((tm, width), lambda i: (i, 1)),
@@ -54,7 +58,7 @@
             full(w_down.shape),
         ],
         out_specs=(
-            pl.BlockSpec((1, tm, 4 * f), lambda i: (i, 0, 0)),
+            pl.BlockSpec((split, part, 4 * f), lambda i: (i, 0, 0)),
             pl.BlockSpec((tm, width), lambda i: (i, 0)),
         ),
         compiler_params=pltpu.CompilerParams(vmem_limit_bytes=48 * 1024 * 1024),

time: 325 us -> 325 us (level)
  no operation moved by 1% of the time
where the time goes in v9:
time: 325 us
  waiting for transfers between devices  203 us (62%)
  blocking collectives  59.9 us (18%)
  Pallas kernels  23.4 us (7%)
  between operations  13.5 us (4%)
  starting transfers between devices  8.24 us (3%)
  matrix products  6.54 us (2%)
  other arithmetic  5.36 us (2%)
  local copies, waits for them, and re-layouts  4.53 us (1%)
    reduce_scatter x1, waiting for transfers between devices, body(): lax.psum_scatter(parts, 'tensor', scatter_dimension=0, tiled=True)[0]  170 us
    all_to_all x2, blocking collectives, gather_tensor(): got = lax.all_to_all(repeated, axis, 0, 0, tiled=True)  59.9 us
    all_gather x1, waiting for transfers between devices, body(): lax.all_gather(jnp.concatenate([tokens, cotangent], axis=1), 'seq', axis=...  27.7 us
    pallas_call x1, Pallas kernels, products(): pl.pallas_call(products_kernel, out_shape=(jax.ShapeDtypeStruct((blocks,...  23.4 us
    ppermute x3, starting transfers between devices, butterfly_sum(): x = x + lax.ppermute(x, axis, [(i, i ^ bit) for i in range(n)])  8.2 us
    dot_general x1, matrix products, body(): lax.dot_general(normed, gather_tensor(second, 'tensor'), (((0,), (0,)), (...  6.54 us
  transfers between devices with their start and end apart: 5, of which 5 were waited for; matrix products, arithmetic and copies ran while one was open for 0% of the time, Pallas kernels for 0%

profile of v9, /device:TPU:0, one launch (start us, length us, event | category | flops | bytes accessed | tf_op | source)
XLA Modules:
  0.0 325.0 jit_solution(3415268890100914826)
XLA Ops:
  6.5 0.0 all-gather.2.cloned.1.call-start
  6.5 1.9 pad_maximum_fusion
  8.4 0.0 all-gather.2.cloned.1.call-update
  8.4 0.0 reduce-scatter.2.cloned.1.call-start
  8.5 1.1 multiply_reduce_fusion
  9.6 3.2 collective-permute-start
  12.8 1.9 collective-permute-done
  14.7 1.7 collective-permute-start.1
  16.4 1.9 collective-permute-done.1
  18.3 3.3 %collective-permute-start.2 = (f32[128]{0:T(128)S(1)}, f32[128]{0:T(128)S(1)}, u32[]{:S(2)}, u32[]{:S(2)}) collective-permute-start(f32[128]{0:T(128)S(1)} %add.24), channel_id=1, source_target_pairs={{0,4},{1,5},{2,6},{3,7},{4,0},{5,1},{6,2},{7,3},{8,12},{9,13},{10,... | collective-permute-start | bytes 1544 | tf_op jit(solution)/shard_map/ppermute | solution.py:84
  21.6 1.8 collective-permute-done.2
  23.4 12.3 %all_to_all.11 = f32[16,1,128]{2,1,0:T(1,128)S(1)} all-to-all(f32[16,1,128]{2,1,0:T(1,128)S(1)} %broadcast_in_dim.4), channel_id=1, replica_groups=mesh['seq'=16,'tensor'=8] {'seq'}, dimensions={0} | all-to-all | bytes 16384 | tf_op jit(solution)/shard_map/all_to_all | solution.py:76
  35.7 0.4 copy.9.inv_ref
  36.1 27.7 %all-gather.2.cloned.1.call-done.t_ref.c_ref = bf16[2048,2048]{1,0:T(8,128)(2,1)} async-done(((bf16[128,2048]{1,0:T(8,128)(2,1)}), bf16[2048,2048]{1,0:T(8,128)(2,1)}) %all-gather.2.cloned.1.call-update) | async-done | bytes 8388624 | tf_op jit(solution)/shard_map/all_gather | solution.py:92
  63.7 0.0 copy-start
  63.7 1.5 copy-done
  65.2 0.0 copy-start.1
  65.2 1.5 copy-done.1
  66.7 0.0 copy-start.2
  66.7 0.7 copy-done.2
  67.4 23.4 %shard_map.73 = (bf16[8,256,3584]{2,1,0:T(8,128)(2,1)}, bf16[2048,1024]{1,0:T(8,128)(2,1)}) custom-call(bf16[2048,2048]{1,0:T(8,128)(2,1)} %all-gather.2.cloned.1.call-done.t_ref.c_ref, bf16[2048,2048]{1,0:T(8,128)(2,1)} %all-gather.2.cloned.1.call-done.t_ref.c_ref, f32[2048,1]{1,0:T(8,128)S(1)} %copy.9.inv_ref, f32[1,1024]{1,0:T(1,128)S(1)} %bitcast.8, ...), custom_call_target="tpu_custom_call" | custom-call | flops 15032385536 | bytes 34603008 | tf_op jit(solution)/shard_map/pallas_call | solution.py:43
  90.9 0.0 reduce-scatter.2.cloned.1.call-update
  90.9 170.2 %reduce-scatter.2.cloned.1.call-done = bf16[1,256,3584]{2,1,0:T(8,128)(2,1)} async-done(((bf16[8,256,3584]{2,1,0:T(8,128)(2,1)}), bf16[1,256,3584]{2,1,0:T(8,128)(2,1)}) %reduce-scatter.2.cloned.1.call-update) | async-done | bytes 1835024 | tf_op jit(solution)/shard_map/reduce_scatter | solution.py:99
  261.1 1.9 bitcast_convert_fusion
  263.0 0.5 fusion.3
  263.5 0.5 broadcast_in_dim.5
  264.0 0.0 copy-start.3
  264.0 47.6 %all_to_all.12 = bf16[8,256,896]{2,1,0:T(8,128)(2,1)S(1)} all-to-all(bf16[8,256,896]{2,1,0:T(8,128)(2,1)S(1)} %broadcast_in_dim.5), channel_id=1, replica_groups=mesh['seq'=16,'tensor'=8] {'tensor'}, dimensions={0} | all-to-all | bytes 7340032 | tf_op jit(solution)/shard_map/all_to_all | solution.py:76
  311.6 0.0 copy-done.3
  311.6 6.5 %convolution_multiply_fusion = f32[1024,896]{1,0:T(8,128)} fusion(bf16[2048,1024]{1,0:T(8,128)(2,1)S(1)} %copy-done.3, bf16[2048,896]{1,0:T(8,128)(2,1)S(1)} %bitcast.9), kind=kOutput, calls=%fused_computation | convolution fusion | flops 3759013888 | bytes 11534336 | tf_op jit(solution)/shard_map/dot_general | solution.py:106
  (4 shorter events, 0.0 us)
Async XLA Ops:
  6.5 57.2 %all-gather.2.cloned.1.call-start = ((), (), s32[]{:S(2)}) async-start(), calls=%async_computation.3 | async-start | bytes 8912896 | tf_op jit(solution)/shard_map/all_gather | solution.py:92
  8.4 252.7 %reduce-scatter.2.cloned.1.call-start = ((), (), s32[]{:S(2)}) async-start(), calls=%async_computation.4 | async-start | bytes 16515072 | tf_op jit(solution)/shard_map/reduce_scatter | solution.py:99
  9.6 5.1 %collective-permute-start = (f32[128]{0:T(128)S(1)}, f32[128]{0:T(128)S(1)}, u32[]{:S(2)}, u32[]{:S(2)}) collective-permute-start(f32[128]{0:T(128)S(1)} %multiply_reduce_fusion), channel_id=1, source_target_pairs={{0,1},{1,0},{2,3},{3,2},{4,5},{5,4},{6,7},{7,6},{8,9},{9,8},{10,11... | collective-permute-start | bytes 1544 | tf_op jit(solution)/shard_map/ppermute | solution.py:84
  14.7 3.6 %collective-permute-start.1 = (f32[128]{0:T(128)S(1)}, f32[128]{0:T(128)S(1)}, u32[]{:S(2)}, u32[]{:S(2)}) collective-permute-start(f32[128]{0:T(128)S(1)} %add.23), channel_id=1, source_target_pairs={{0,2},{1,3},{2,0},{3,1},{4,6},{5,7},{6,4},{7,5},{8,10},{9,11},{10,... | collective-permute-start | bytes 1544 | tf_op jit(solution)/shard_map/ppermute | solution.py:84
  18.3 5.1 %collective-permute-start.2 = (f32[128]{0:T(128)S(1)}, f32[128]{0:T(128)S(1)}, u32[]{:S(2)}, u32[]{:S(2)}) collective-permute-start(f32[128]{0:T(128)S(1)} %add.24), channel_id=1, source_target_pairs={{0,4},{1,5},{2,6},{3,7},{4,0},{5,1},{6,2},{7,3},{8,12},{9,13},{10,... | collective-permute-start | bytes 1544 | tf_op jit(solution)/shard_map/ppermute | solution.py:84
  63.7 1.5 copy-start
  65.2 1.5 copy-start.1
  66.7 0.7 copy-start.2
  264.0 47.6 %copy-start.3 = (bf16[2048,1024]{1,0:T(8,128)(2,1)S(1)}, bf16[2048,1024]{1,0:T(8,128)(2,1)}, u32[]{:S(2)}) copy-start(bf16[2048,1024]{1,0:T(8,128)(2,1)} %get-tuple-element.7) | copy-start | bytes 12582916
Sparse Core Ops, SparseCore 0:
  9.0 54.6 all-gather.1
  91.0 170.0 reduce-scatter.1

commit v10 on v6

--- a/solution.py
+++ b/solution.py
@@ -66,6 +66,24 @@
     )(both, both, inverse.reshape(rows, 1), gain.reshape(1, width), w_gate, w_up, probe, w_down)
 
 
+def second_kernel(s_ref, o_ref):
+    f = o_ref.shape[2]
+    x = s_ref[0].astype(jnp.float32)
+    second = second_factor(x[:, :f], x[:, f:2 * f], x[:, 2 * f:3 * f], x[:, 3 * f:])
+    for j in range(o_ref.shape[0]):
+        o_ref[j] = second
+
+
+def second_repeated(summed, copies):
+    rows, f = summed.shape[1], summed.shape[2] // 4
+    return pl.pallas_call(
+        second_kernel,
+        out_shape=jax.ShapeDtypeStruct((copies, rows, f), jnp.bfloat16),
+        in_specs=[pl.BlockSpec(memory_space=pltpu.VMEM)],
+        out_specs=pl.BlockSpec(memory_space=pltpu.VMEM),
+    )(summed)
+
+
 def gather_tensor(x, axis):
     n = lax.axis_size(axis)
     repeated = jnp.broadcast_to(x[None], (n,) + x.shape)
@@ -92,16 +110,12 @@
     total_tokens = both.shape[0]
     unit_count = w_gate.shape[1]
     parts, normed = products(both, inverse, gain, w_gate, w_up, probe, w_down, n_tensor)
-    summed = lax.psum_scatter(parts, "tensor", scatter_dimension=0, tiled=True)[0].astype(jnp.float32)
-    second = second_factor(
-        summed[:, :unit_count],
-        summed[:, unit_count : 2 * unit_count],
-        summed[:, 2 * unit_count : 3 * unit_count],
-        summed[:, 3 * unit_count :],
-    )
+    summed = lax.psum_scatter(parts, "tensor", scatter_dimension=0, tiled=True)
+    repeated = second_repeated(summed, n_tensor)
+    gathered = lax.all_to_all(repeated, "tensor", 0, 0, tiled=True)
     product = lax.dot_general(
         normed,
-        gather_tensor(second, "tensor"),
+        gathered.reshape(-1, unit_count),
         (((0,), (0,)), ((), ())),
         preferred_element_type=jnp.float32,
     )

time: 325 us -> 327 us (level)
  Pallas kernels: 23.4 us -> 27.3 us
    all_to_all x0 -> x1, blocking collectives: none -> 48.7 us  [body(): gathered = lax.all_to_all(repeated, 'tensor', 0, 0, tiled=True)]
    all_to_all x2 -> x1, blocking collectives: 59.9 us -> 12.3 us  [gather_tensor(): got = lax.all_to_all(repeated, axis, 0, 0, tiled=True)]
    pallas_call x0 -> x1, Pallas kernels: none -> 3.84 us  [second_repeated(): pl.pallas_call(second_kernel, out_shape=jax.ShapeDtypeStruct((copies, row...]
where the time goes in v10:
time: 327 us
  waiting for transfers between devices  203 us (62%)
  blocking collectives  61 us (19%)
  Pallas kernels  27.3 us (8%)
  between operations  13.4 us (4%)
  starting transfers between devices  8.24 us (3%)
  matrix products  6.54 us (2%)
  local copies, waits for them, and re-layouts  4.06 us (1%)
    reduce_scatter x1, waiting for transfers between devices, body(): summed = lax.psum_scatter(parts, 'tensor', scatter_dimension=0, tiled=True)  170 us
    all_to_all x1, blocking collectives, body(): gathered = lax.all_to_all(repeated, 'tensor', 0, 0, tiled=True)  48.7 us
    all_gather x1, waiting for transfers between devices, body(): lax.all_gather(jnp.concatenate([tokens, cotangent], axis=1), 'seq', axis=...  27.7 us
    pallas_call x1, Pallas kernels, products(): pl.pallas_call(products_kernel, out_shape=(jax.ShapeDtypeStruct((blocks,...  23.4 us
    all_to_all x1, blocking collectives, gather_tensor(): got = lax.all_to_all(repeated, axis, 0, 0, tiled=True)  12.3 us
    ppermute x3, starting transfers between devices, butterfly_sum(): x = x + lax.ppermute(x, axis, [(i, i ^ bit) for i in range(n)])  8.2 us
  transfers between devices with their start and end apart: 5, of which 5 were waited for; matrix products, arithmetic and copies ran while one was open for 0% of the time, Pallas kernels for 0%

profile of v10, /device:TPU:0, one launch (start us, length us, event | category | flops | bytes accessed | tf_op | source)
XLA Modules:
  0.0 327.0 jit_solution(4276892887934362103)
XLA Ops:
  6.5 0.0 all-gather.2.cloned.1.call-start
  6.5 1.9 pad_maximum_fusion
  8.4 0.0 all-gather.2.cloned.1.call-update
  8.4 0.0 reduce-scatter.2.cloned.1.call-start
  8.5 1.1 multiply_reduce_fusion
  9.6 3.2 collective-permute-start
  12.8 1.9 collective-permute-done
  14.7 1.7 collective-permute-start.1
  16.4 1.9 collective-permute-done.1
  18.3 3.3 %collective-permute-start.2 = (f32[128]{0:T(128)S(1)}, f32[128]{0:T(128)S(1)}, u32[]{:S(2)}, u32[]{:S(2)}) collective-permute-start(f32[128]{0:T(128)S(1)} %add.18), channel_id=1, source_target_pairs={{0,4},{1,5},{2,6},{3,7},{4,0},{5,1},{6,2},{7,3},{8,12},{9,13},{10,... | collective-permute-start | bytes 1544 | tf_op jit(solution)/shard_map/ppermute | solution.py:98
  21.6 1.8 collective-permute-done.2
  23.4 12.3 %all_to_all.11 = f32[16,1,128]{2,1,0:T(1,128)S(1)} all-to-all(f32[16,1,128]{2,1,0:T(1,128)S(1)} %broadcast_in_dim.2), channel_id=1, replica_groups=mesh['seq'=16,'tensor'=8] {'seq'}, dimensions={0} | all-to-all | bytes 16384 | tf_op jit(solution)/shard_map/all_to_all | solution.py:90
  35.7 0.4 copy.9.inv_ref
  36.1 27.7 %all-gather.2.cloned.1.call-done.t_ref.c_ref = bf16[2048,2048]{1,0:T(8,128)(2,1)} async-done(((bf16[128,2048]{1,0:T(8,128)(2,1)}), bf16[2048,2048]{1,0:T(8,128)(2,1)}) %all-gather.2.cloned.1.call-update) | async-done | bytes 8388624 | tf_op jit(solution)/shard_map/all_gather | solution.py:106
  63.7 0.0 copy-start
  63.7 1.5 copy-done
  65.2 0.0 copy-start.1
  65.2 1.5 copy-done.1
  66.7 0.0 copy-start.2
  66.7 0.7 copy-done.2
  67.4 23.4 %shard_map.73 = (bf16[8,256,3584]{2,1,0:T(8,128)(2,1)}, bf16[2048,1024]{1,0:T(8,128)(2,1)}) custom-call(bf16[2048,2048]{1,0:T(8,128)(2,1)} %all-gather.2.cloned.1.call-done.t_ref.c_ref, bf16[2048,2048]{1,0:T(8,128)(2,1)} %all-gather.2.cloned.1.call-done.t_ref.c_ref, f32[2048,1]{1,0:T(8,128)S(1)} %copy.9.inv_ref, f32[1,1024]{1,0:T(1,128)S(1)} %bitcast.5, ...), custom_call_target="tpu_custom_call" | custom-call | flops 15032385536 | bytes 34603008 | tf_op jit(solution)/shard_map/pallas_call | solution.py:39
  90.9 0.0 reduce-scatter.2.cloned.1.call-update
  90.9 170.2 %reduce-scatter.2.cloned.1.call-done.s_ref = bf16[1,256,3584]{2,1,0:T(8,128)(2,1)} async-done(((bf16[8,256,3584]{2,1,0:T(8,128)(2,1)}), bf16[1,256,3584]{2,1,0:T(8,128)(2,1)}) %reduce-scatter.2.cloned.1.call-update) | async-done | bytes 1835024 | tf_op jit(solution)/shard_map/reduce_scatter | solution.py:113
  261.1 3.8 %shard_map.74 = bf16[8,256,896]{2,1,0:T(8,128)(2,1)} custom-call(bf16[1,256,3584]{2,1,0:T(8,128)(2,1)} %reduce-scatter.2.cloned.1.call-done.s_ref), custom_call_target="tpu_custom_call" | custom-call | tf_op jit(solution)/shard_map/pallas_call | solution.py:79
  264.9 0.0 copy-start.3
  264.9 48.7 %all_to_all.12 = bf16[8,256,896]{2,1,0:T(8,128)(2,1)S(1)} all-to-all(bf16[8,256,896]{2,1,0:T(8,128)(2,1)} %shard_map.74), channel_id=1, replica_groups=mesh['seq'=16,'tensor'=8] {'tensor'}, dimensions={0} | all-to-all | bytes 7340032 | tf_op jit(solution)/shard_map/all_to_all | solution.py:115
  313.6 0.0 copy-done.3
  313.6 6.5 %convolution_multiply_fusion = f32[1024,896]{1,0:T(8,128)} fusion(bf16[2048,1024]{1,0:T(8,128)(2,1)S(1)} %copy-done.3, bf16[2048,896]{1,0:T(8,128)(2,1)S(1)} %bitcast.6), kind=kOutput, calls=%fused_computation | convolution fusion | flops 3759013888 | bytes 11534336 | tf_op jit(solution)/shard_map/dot_general | solution.py:116
  (4 shorter events, 0.0 us)
Async XLA Ops:
  6.5 57.2 %all-gather.2.cloned.1.call-start = ((), (), s32[]{:S(2)}) async-start(), calls=%async_computation.3 | async-start | bytes 8912896 | tf_op jit(solution)/shard_map/all_gather | solution.py:106
  8.4 252.7 %reduce-scatter.2.cloned.1.call-start = ((), (), s32[]{:S(2)}) async-start(), calls=%async_computation.4 | async-start | bytes 16515072 | tf_op jit(solution)/shard_map/reduce_scatter | solution.py:113
  9.6 5.1 %collective-permute-start = (f32[128]{0:T(128)S(1)}, f32[128]{0:T(128)S(1)}, u32[]{:S(2)}, u32[]{:S(2)}) collective-permute-start(f32[128]{0:T(128)S(1)} %multiply_reduce_fusion), channel_id=1, source_target_pairs={{0,1},{1,0},{2,3},{3,2},{4,5},{5,4},{6,7},{7,6},{8,9},{9,8},{10,11... | collective-permute-start | bytes 1544 | tf_op jit(solution)/shard_map/ppermute | solution.py:98
  14.7 3.6 %collective-permute-start.1 = (f32[128]{0:T(128)S(1)}, f32[128]{0:T(128)S(1)}, u32[]{:S(2)}, u32[]{:S(2)}) collective-permute-start(f32[128]{0:T(128)S(1)} %add.17), channel_id=1, source_target_pairs={{0,2},{1,3},{2,0},{3,1},{4,6},{5,7},{6,4},{7,5},{8,10},{9,11},{10,... | collective-permute-start | bytes 1544 | tf_op jit(solution)/shard_map/ppermute | solution.py:98
  18.3 5.1 %collective-permute-start.2 = (f32[128]{0:T(128)S(1)}, f32[128]{0:T(128)S(1)}, u32[]{:S(2)}, u32[]{:S(2)}) collective-permute-start(f32[128]{0:T(128)S(1)} %add.18), channel_id=1, source_target_pairs={{0,4},{1,5},{2,6},{3,7},{4,0},{5,1},{6,2},{7,3},{8,12},{9,13},{10,... | collective-permute-start | bytes 1544 | tf_op jit(solution)/shard_map/ppermute | solution.py:98
  63.7 1.5 copy-start
  65.2 1.5 copy-start.1
  66.7 0.7 copy-start.2
  264.9 48.7 %copy-start.3 = (bf16[2048,1024]{1,0:T(8,128)(2,1)S(1)}, bf16[2048,1024]{1,0:T(8,128)(2,1)}, u32[]{:S(2)}) copy-start(bf16[2048,1024]{1,0:T(8,128)(2,1)} %get-tuple-element.7) | copy-start | bytes 12582916
Sparse Core Ops, SparseCore 0:
  9.0 54.6 all-gather.1
  91.0 170.0 reduce-scatter.1

commit v11 on v6

--- a/solution.py
+++ b/solution.py
@@ -57,7 +57,6 @@
             pl.BlockSpec((1, tm, 4 * f), lambda i: (i, 0, 0)),
             pl.BlockSpec((tm, width), lambda i: (i, 0)),
         ),
-        compiler_params=pltpu.CompilerParams(vmem_limit_bytes=48 * 1024 * 1024),
         cost_estimate=pl.CostEstimate(
             flops=2 * rows * width * f * 4,
             transcendentals=0,

time: 325 us -> 323 us (level)
    unnamed x8 -> x2, local copies, waits for them, and re-layouts: 3.69 us -> 0.01 us
  transfers between devices with their start and end apart: 5 -> 5, of which waited for: 5 -> 5; matrix products, arithmetic and copies ran while one was open for 0% -> 1% of each run, Pallas kernels for 0% -> 0%
where the time goes in v11:
time: 323 us
  waiting for transfers between devices  203 us (63%)
  blocking collectives  59.9 us (19%)
  Pallas kernels  24.8 us (8%)
  between operations  13.4 us (4%)
  starting transfers between devices  8.24 us (3%)
  matrix products  6.54 us (2%)
  other arithmetic  5.36 us (2%)
    reduce_scatter x1, waiting for transfers between devices, body(): lax.psum_scatter(parts, 'tensor', scatter_dimension=0, tiled=True)[0]  170 us
    all_to_all x2, blocking collectives, gather_tensor(): got = lax.all_to_all(repeated, axis, 0, 0, tiled=True)  59.9 us
    all_gather x1, waiting for transfers between devices, body(): lax.all_gather(jnp.concatenate([tokens, cotangent], axis=1), 'seq', axis=...  26.7 us
    pallas_call x1, Pallas kernels, products(): pl.pallas_call(products_kernel, out_shape=(jax.ShapeDtypeStruct((blocks,...  24.8 us
    ppermute x3, starting transfers between devices, butterfly_sum(): x = x + lax.ppermute(x, axis, [(i, i ^ bit) for i in range(n)])  8.2 us
    dot_general x1, matrix products, body(): lax.dot_general(normed, gather_tensor(second, 'tensor'), (((0,), (0,)), (...  6.54 us
  transfers between devices with their start and end apart: 5, of which 5 were waited for; matrix products, arithmetic and copies ran while one was open for 1% of the time, Pallas kernels for 0%

profile of v11, /device:TPU:0, one launch (start us, length us, event | category | flops | bytes accessed | tf_op | source)
XLA Modules:
  0.0 322.7 jit_solution(5935533271152745997)
XLA Ops:
  6.5 0.0 all-gather.2.cloned.1.call-start
  6.5 1.9 pad_maximum_fusion
  8.4 0.0 all-gather.2.cloned.1.call-update
  8.4 0.0 reduce-scatter.2.cloned.1.call-start
  8.5 1.1 multiply_reduce_fusion
  9.6 3.2 collective-permute-start
  12.8 1.9 collective-permute-done
  14.7 1.7 collective-permute-start.1
  16.4 1.9 collective-permute-done.1
  18.3 3.3 %collective-permute-start.2 = (f32[128]{0:T(128)S(1)}, f32[128]{0:T(128)S(1)}, u32[]{:S(2)}, u32[]{:S(2)}) collective-permute-start(f32[128]{0:T(128)S(1)} %add.24), channel_id=1, source_target_pairs={{0,4},{1,5},{2,6},{3,7},{4,0},{5,1},{6,2},{7,3},{8,12},{9,13},{10,... | collective-permute-start | bytes 1544 | tf_op jit(solution)/shard_map/ppermute | solution.py:79
  21.6 1.8 collective-permute-done.2
  23.4 12.3 %all_to_all.11 = f32[16,1,128]{2,1,0:T(1,128)S(1)} all-to-all(f32[16,1,128]{2,1,0:T(1,128)S(1)} %broadcast_in_dim.4), channel_id=1, replica_groups=mesh['seq'=16,'tensor'=8] {'seq'}, dimensions={0} | all-to-all | bytes 16384 | tf_op jit(solution)/shard_map/all_to_all | solution.py:71
  35.7 1.3 copy.9.inv_ref
  37.0 26.7 %all-gather.2.cloned.1.call-done.t_ref.c_ref = bf16[2048,2048]{1,0:T(8,128)(2,1)} async-done(((bf16[128,2048]{1,0:T(8,128)(2,1)}), bf16[2048,2048]{1,0:T(8,128)(2,1)}) %all-gather.2.cloned.1.call-update) | async-done | bytes 8388624 | tf_op jit(solution)/shard_map/all_gather | solution.py:87
  63.7 24.8 %shard_map.73 = (bf16[8,256,3584]{2,1,0:T(8,128)(2,1)}, bf16[2048,1024]{1,0:T(8,128)(2,1)}) custom-call(bf16[2048,2048]{1,0:T(8,128)(2,1)} %all-gather.2.cloned.1.call-done.t_ref.c_ref, bf16[2048,2048]{1,0:T(8,128)(2,1)} %all-gather.2.cloned.1.call-done.t_ref.c_ref, f32[2048,1]{1,0:T(8,128)} %copy.9.inv_ref, f32[1,1024]{1,0:T(1,128)} %bitcast.10, ...), custom_call_target="tpu_custom_call" | custom-call | flops 15032385536 | bytes 34603008 | tf_op jit(solution)/shard_map/pallas_call | solution.py:39
  88.6 0.0 reduce-scatter.2.cloned.1.call-update
  88.6 170.2 %reduce-scatter.2.cloned.1.call-done = bf16[1,256,3584]{2,1,0:T(8,128)(2,1)} async-done(((bf16[8,256,3584]{2,1,0:T(8,128)(2,1)}), bf16[1,256,3584]{2,1,0:T(8,128)(2,1)}) %reduce-scatter.2.cloned.1.call-update) | async-done | bytes 1835024 | tf_op jit(solution)/shard_map/reduce_scatter | solution.py:94
  258.8 1.9 bitcast_convert_fusion
  260.8 0.5 fusion.3
  261.3 0.5 broadcast_in_dim.5
  261.7 0.0 copy-start
  261.7 47.6 %all_to_all.12 = bf16[8,256,896]{2,1,0:T(8,128)(2,1)S(1)} all-to-all(bf16[8,256,896]{2,1,0:T(8,128)(2,1)S(1)} %broadcast_in_dim.5), channel_id=1, replica_groups=mesh['seq'=16,'tensor'=8] {'tensor'}, dimensions={0} | all-to-all | bytes 7340032 | tf_op jit(solution)/shard_map/all_to_all | solution.py:71
  309.3 0.0 copy-done
  309.3 6.5 %convolution_multiply_fusion = f32[1024,896]{1,0:T(8,128)} fusion(bf16[2048,1024]{1,0:T(8,128)(2,1)S(1)} %copy-done, bf16[2048,896]{1,0:T(8,128)(2,1)S(1)} %bitcast.8), kind=kOutput, calls=%fused_computation | convolution fusion | flops 3759013888 | bytes 11534336 | tf_op jit(solution)/shard_map/dot_general | solution.py:101
  (4 shorter events, 0.0 us)
Async XLA Ops:
  6.5 57.2 %all-gather.2.cloned.1.call-start = ((), (), s32[]{:S(2)}) async-start(), calls=%async_computation.3 | async-start | bytes 8912896 | tf_op jit(solution)/shard_map/all_gather | solution.py:87
  8.4 250.4 %reduce-scatter.2.cloned.1.call-start = ((), (), s32[]{:S(2)}) async-start(), calls=%async_computation.4 | async-start | bytes 16515072 | tf_op jit(solution)/shard_map/reduce_scatter | solution.py:94
  9.6 5.1 %collective-permute-start = (f32[128]{0:T(128)S(1)}, f32[128]{0:T(128)S(1)}, u32[]{:S(2)}, u32[]{:S(2)}) collective-permute-start(f32[128]{0:T(128)S(1)} %multiply_reduce_fusion), channel_id=1, source_target_pairs={{0,1},{1,0},{2,3},{3,2},{4,5},{5,4},{6,7},{7,6},{8,9},{9,8},{10,11... | collective-permute-start | bytes 1544 | tf_op jit(solution)/shard_map/ppermute | solution.py:79
  14.7 3.6 %collective-permute-start.1 = (f32[128]{0:T(128)S(1)}, f32[128]{0:T(128)S(1)}, u32[]{:S(2)}, u32[]{:S(2)}) collective-permute-start(f32[128]{0:T(128)S(1)} %add.23), channel_id=1, source_target_pairs={{0,2},{1,3},{2,0},{3,1},{4,6},{5,7},{6,4},{7,5},{8,10},{9,11},{10,... | collective-permute-start | bytes 1544 | tf_op jit(solution)/shard_map/ppermute | solution.py:79
  18.3 5.1 %collective-permute-start.2 = (f32[128]{0:T(128)S(1)}, f32[128]{0:T(128)S(1)}, u32[]{:S(2)}, u32[]{:S(2)}) collective-permute-start(f32[128]{0:T(128)S(1)} %add.24), channel_id=1, source_target_pairs={{0,4},{1,5},{2,6},{3,7},{4,0},{5,1},{6,2},{7,3},{8,12},{9,13},{10,... | collective-permute-start | bytes 1544 | tf_op jit(solution)/shard_map/ppermute | solution.py:79
  261.7 47.6 %copy-start = (bf16[2048,1024]{1,0:T(8,128)(2,1)S(1)}, bf16[2048,1024]{1,0:T(8,128)(2,1)}, u32[]{:S(2)}) copy-start(bf16[2048,1024]{1,0:T(8,128)(2,1)} %get-tuple-element.7) | copy-start | bytes 12582916
Sparse Core Ops, SparseCore 0:
  9.0 54.6 all-gather.1
  88.7 170.0 reduce-scatter.1

commit v12 on v11

--- a/solution.py
+++ b/solution.py
@@ -20,21 +20,26 @@
 
 def products_kernel(t_ref, c_ref, inv_ref, gain_ref, wg_ref, wu_ref, pr_ref, wd_ref, o_ref, n_out_ref):
     f = wg_ref.shape[1]
-    n = (t_ref[...].astype(jnp.float32) * inv_ref[...] * gain_ref[...]).astype(jnp.bfloat16)
+    rows = n_out_ref.shape[0]
+    t = t_ref[...].reshape(rows, t_ref.shape[-1])
+    n = (t.astype(jnp.float32) * inv_ref[...] * gain_ref[...]).astype(jnp.bfloat16)
     n_out_ref[...] = n
     for p, w_ref in enumerate((wg_ref, wu_ref, pr_ref)):
         o_ref[0, :, p * f:(p + 1) * f] = jnp.dot(
             n, w_ref[...], preferred_element_type=jnp.float32
         ).astype(o_ref.dtype)
     o_ref[0, :, 3 * f:4 * f] = lax.dot_general(
-        c_ref[...], wd_ref[...], (((1,), (1,)), ((), ())), preferred_element_type=jnp.float32
+        c_ref[...].reshape(rows, c_ref.shape[-1]), wd_ref[...], (((1,), (1,)), ((), ())),
+        preferred_element_type=jnp.float32
     ).astype(o_ref.dtype)
 
 
 def products(both, inverse, gain, w_gate, w_up, probe, w_down, blocks):
-    rows, width = both.shape[0], both.shape[1] // 2
+    seqs, _, local, width = both.shape
+    rows = seqs * local
     f = w_gate.shape[1]
     tm = rows // blocks
+    per = tm // local
     full = lambda shape: pl.BlockSpec(shape, lambda i: (0, 0))
     return pl.pallas_call(
         products_kernel,
@@ -44,8 +49,8 @@
         ),
         grid=(blocks,),
         in_specs=[
-            pl.BlockSpec((tm, width), lambda i: (i, 0)),
-            pl.BlockSpec((tm, width), lambda i: (i, 1)),
+            pl.BlockSpec((per, 1, local, width), lambda i: (i, 0, 0, 0)),
+            pl.BlockSpec((per, 1, local, width), lambda i: (i, 1, 0, 0)),
             pl.BlockSpec((tm, 1), lambda i: (i, 0)),
             full((1, width)),
             full(w_gate.shape),
@@ -84,11 +89,13 @@
 def body(tokens, cotangent, gain, w_gate, w_up, w_down, probe):
     n_tensor = lax.axis_size("tensor")
     width = tokens.shape[1]
-    both = lax.all_gather(jnp.concatenate([tokens, cotangent], axis=1), "seq", axis=0, tiled=True)
+    local_rows = tokens.shape[0]
+    both = lax.all_gather(jnp.concatenate([tokens, cotangent], axis=0), "seq", axis=0, tiled=True)
+    both = both.reshape(-1, 2, local_rows, width)
     values = tokens.astype(jnp.float32)
     squares = butterfly_sum(jnp.sum(values * values, axis=1), "tensor")
     inverse = gather_tensor(lax.rsqrt(squares / D + epsilon), "seq")
-    total_tokens = both.shape[0]
+    total_tokens = both.shape[0] * local_rows
     unit_count = w_gate.shape[1]
     parts, normed = products(both, inverse, gain, w_gate, w_up, probe, w_down, n_tensor)
     summed = lax.psum_scatter(parts, "tensor", scatter_dimension=0, tiled=True)[0].astype(jnp.float32)

time: 323 us -> 323 us (level)
  no operation moved by 1% of the time
where the time goes in v12:
time: 323 us
  waiting for transfers between devices  203 us (63%)
  blocking collectives  59.9 us (19%)
  Pallas kernels  24.7 us (8%)
  between operations  13.4 us (4%)
  starting transfers between devices  8.24 us (3%)
  matrix products  6.54 us (2%)
  other arithmetic  5.35 us (2%)
    reduce_scatter x1, waiting for transfers between devices, body(): lax.psum_scatter(parts, 'tensor', scatter_dimension=0, tiled=True)[0]  170 us
    all_to_all x2, blocking collectives, gather_tensor(): got = lax.all_to_all(repeated, axis, 0, 0, tiled=True)  59.9 us
    all_gather x1, waiting for transfers between devices, body(): lax.all_gather(jnp.concatenate([tokens, cotangent], axis=0), 'seq', axis=...  26.7 us
    pallas_call x1, Pallas kernels, products(): pl.pallas_call(products_kernel, out_shape=(jax.ShapeDtypeStruct((blocks,...  24.7 us
    ppermute x3, starting transfers between devices, butterfly_sum(): x = x + lax.ppermute(x, axis, [(i, i ^ bit) for i in range(n)])  8.2 us
    dot_general x1, matrix products, body(): lax.dot_general(normed, gather_tensor(second, 'tensor'), (((0,), (0,)), (...  6.54 us
  transfers between devices with their start and end apart: 5, of which 5 were waited for; matrix products, arithmetic and copies ran while one was open for 1% of the time, Pallas kernels for 0%

profile of v12, /device:TPU:0, one launch (start us, length us, event | category | flops | bytes accessed | tf_op | source)
XLA Modules:
  0.0 322.7 jit_solution(7852391886120874893)
XLA Ops:
  6.5 0.0 all-gather.2.cloned.1.call-start
  6.5 1.8 pad_maximum_fusion
  8.4 0.0 all-gather.2.cloned.1.call-update
  8.4 0.0 reduce-scatter.2.cloned.1.call-start
  8.5 1.1 multiply_reduce_fusion
  9.5 3.2 collective-permute-start
  12.8 1.9 collective-permute-done
  14.7 1.7 collective-permute-start.1
  16.4 1.9 collective-permute-done.1
  18.3 3.3 %collective-permute-start.2 = (f32[128]{0:T(128)S(1)}, f32[128]{0:T(128)S(1)}, u32[]{:S(2)}, u32[]{:S(2)}) collective-permute-start(f32[128]{0:T(128)S(1)} %add.24), channel_id=1, source_target_pairs={{0,4},{1,5},{2,6},{3,7},{4,0},{5,1},{6,2},{7,3},{8,12},{9,13},{10,... | collective-permute-start | bytes 1544 | tf_op jit(solution)/shard_map/ppermute | solution.py:84
  21.6 1.8 collective-permute-done.2
  23.4 12.3 %all_to_all.11 = f32[16,1,128]{2,1,0:T(1,128)S(1)} all-to-all(f32[16,1,128]{2,1,0:T(1,128)S(1)} %broadcast_in_dim.4), channel_id=1, replica_groups=mesh['seq'=16,'tensor'=8] {'seq'}, dimensions={0} | all-to-all | bytes 16384 | tf_op jit(solution)/shard_map/all_to_all | solution.py:76
  35.7 1.3 copy.9.inv_ref
  37.0 26.7 %all-gather.2.cloned.1.call-done = bf16[4096,1024]{1,0:T(8,128)(2,1)} async-done(((bf16[256,1024]{1,0:T(8,128)(2,1)}), bf16[4096,1024]{1,0:T(8,128)(2,1)}) %all-gather.2.cloned.1.call-update) | async-done | bytes 8388624 | tf_op jit(solution)/shard_map/all_gather | solution.py:93
  63.7 24.7 %shard_map.73 = (bf16[8,256,3584]{2,1,0:T(8,128)(2,1)}, bf16[2048,1024]{1,0:T(8,128)(2,1)}) custom-call(bf16[16,2,128,1024]{3,2,1,0:T(8,128)(2,1)} %bitcast.11, bf16[16,2,128,1024]{3,2,1,0:T(8,128)(2,1)} %bitcast.12, f32[2048,1]{1,0:T(8,128)} %copy.9.inv_ref, f32[1,1024]{1,0:T(1,128)} %bitcast.13, bf16[1024,896]{1,0:T(8,128)(2,1)} %wg_ref.1, ...), custom_call_target="tpu_custom_call" | custom-call | flops 15032385536 | bytes 34603008 | tf_op jit(solution)/shard_map/pallas_call | solution.py:44
  88.5 0.0 reduce-scatter.2.cloned.1.call-update
  88.5 170.3 %reduce-scatter.2.cloned.1.call-done = bf16[1,256,3584]{2,1,0:T(8,128)(2,1)} async-done(((bf16[8,256,3584]{2,1,0:T(8,128)(2,1)}), bf16[1,256,3584]{2,1,0:T(8,128)(2,1)}) %reduce-scatter.2.cloned.1.call-update) | async-done | bytes 1835024 | tf_op jit(solution)/shard_map/reduce_scatter | solution.py:101
  258.8 1.9 bitcast_convert_fusion
  260.7 0.5 fusion.3
  261.2 0.5 broadcast_in_dim.5
  261.7 0.0 copy-start
  261.7 47.6 %all_to_all.12 = bf16[8,256,896]{2,1,0:T(8,128)(2,1)S(1)} all-to-all(bf16[8,256,896]{2,1,0:T(8,128)(2,1)S(1)} %broadcast_in_dim.5), channel_id=1, replica_groups=mesh['seq'=16,'tensor'=8] {'tensor'}, dimensions={0} | all-to-all | bytes 7340032 | tf_op jit(solution)/shard_map/all_to_all | solution.py:76
  309.3 0.0 copy-done
  309.3 6.5 %convolution_multiply_fusion = f32[1024,896]{1,0:T(8,128)} fusion(bf16[2048,1024]{1,0:T(8,128)(2,1)S(1)} %copy-done, bf16[2048,896]{1,0:T(8,128)(2,1)S(1)} %bitcast.9), kind=kOutput, calls=%fused_computation | convolution fusion | flops 3759013888 | bytes 11534336 | tf_op jit(solution)/shard_map/dot_general | solution.py:108
  (4 shorter events, 0.0 us)
Async XLA Ops:
  6.5 57.2 %all-gather.2.cloned.1.call-start = ((), (), s32[]{:S(2)}) async-start(), calls=%async_computation.3 | async-start | bytes 8912896 | tf_op jit(solution)/shard_map/all_gather | solution.py:93
  8.4 250.4 %reduce-scatter.2.cloned.1.call-start = ((), (), s32[]{:S(2)}) async-start(), calls=%async_computation.4 | async-start | bytes 16515072 | tf_op jit(solution)/shard_map/reduce_scatter | solution.py:101
  9.5 5.1 %collective-permute-start = (f32[128]{0:T(128)S(1)}, f32[128]{0:T(128)S(1)}, u32[]{:S(2)}, u32[]{:S(2)}) collective-permute-start(f32[128]{0:T(128)S(1)} %multiply_reduce_fusion), channel_id=1, source_target_pairs={{0,1},{1,0},{2,3},{3,2},{4,5},{5,4},{6,7},{7,6},{8,9},{9,8},{10,11... | collective-permute-start | bytes 1544 | tf_op jit(solution)/shard_map/ppermute | solution.py:84
  14.7 3.6 %collective-permute-start.1 = (f32[128]{0:T(128)S(1)}, f32[128]{0:T(128)S(1)}, u32[]{:S(2)}, u32[]{:S(2)}) collective-permute-start(f32[128]{0:T(128)S(1)} %add.23), channel_id=1, source_target_pairs={{0,2},{1,3},{2,0},{3,1},{4,6},{5,7},{6,4},{7,5},{8,10},{9,11},{10,... | collective-permute-start | bytes 1544 | tf_op jit(solution)/shard_map/ppermute | solution.py:84
  18.3 5.1 %collective-permute-start.2 = (f32[128]{0:T(128)S(1)}, f32[128]{0:T(128)S(1)}, u32[]{:S(2)}, u32[]{:S(2)}) collective-permute-start(f32[128]{0:T(128)S(1)} %add.24), channel_id=1, source_target_pairs={{0,4},{1,5},{2,6},{3,7},{4,0},{5,1},{6,2},{7,3},{8,12},{9,13},{10,... | collective-permute-start | bytes 1544 | tf_op jit(solution)/shard_map/ppermute | solution.py:84
  261.7 47.6 %copy-start = (bf16[2048,1024]{1,0:T(8,128)(2,1)S(1)}, bf16[2048,1024]{1,0:T(8,128)(2,1)}, u32[]{:S(2)}) copy-start(bf16[2048,1024]{1,0:T(8,128)(2,1)} %get-tuple-element.7) | copy-start | bytes 12582916
Sparse Core Ops, SparseCore 0:
  9.0 54.6 all-gather.1
  88.6 170.1 reduce-scatter.1
